TPU v7x, 256 devices: a whole 4x4x8 slice. The times are simulated.
256 devices in a mesh: grp: 4 (over z_lo, core), row: 4 (over z_hi), col: 16 (over x, y).
Axes of the slice: x: 4, y: 4, z: 8 (z_hi: 4, z_lo: 2; z = z_hi * 2 + z_lo), core: 2. Of those that a mesh axis runs over, the one named last changes fastest.
Arguments:
- pair_rep: bfloat16 [512, 512, 128], P('row', ('grp', 'col')), may hold values from -20 to 20
- residue_index: int32 [512], replicated, may hold values from 0 to 63
- chain_index: int32 [512], replicated, may hold values from 0 to 3, never falling along the last dimension, each value on 1 to 256 neighbouring positions
- token_mask: int32 [512], replicated, may hold values 0 or 1
- relpos_table: bfloat16 [66, 128], replicated, may hold values from -5 to 5
- proj_in: bfloat16 [128, 640], replicated, may hold values from -0.5 to 0.5
- out_proj: bfloat16 [128, 128], replicated, may hold values from -0.5 to 0.5
- bias_weight: float32 [128, 16], replicated, may hold values from -2 to 2
- single_rep: bfloat16 [48, 512, 768], P('col', 'row'), may hold values from -6 to 6
- w_qkvg: bfloat16 [4, 768, 768], P(None, None, 'grp'), may hold values from -0.21875 to 0.21875
- w_out: bfloat16 [768, 768], P('grp'), may hold values from -0.21875 to 0.21875
- cotangent: bfloat16 [48, 512, 768], P('col', 'row'), may hold values from -6 to 6
Outputs:
- pair_out: bfloat16 [512, 512, 128], P('row', ('grp', 'col'))
- single_out: bfloat16 [48, 512, 768], P('col', 'row')
- bias_grad: float32 [16, 512, 512], P('grp', 'row', 'col')
All inputs are finite; a program needn't handle non-finite values.
Results may differ from a plain program's by a relative error of at most 0.014.
Values may be sent and summed in bfloat16 or wider, within the bound.
No kernel may reach another device: no remote copies, remote signals or barrier semaphores. Data moves between devices by JAX's collectives and lax.ppermute only.
A program may use at most 64 MiB of HBM per device.

v0:
```python
import math

import jax
import jax.numpy as jnp
from jax import lax
from jax.experimental import pallas as pl
from jax.experimental.pallas import tpu as pltpu
from jax.sharding import PartitionSpec as P

BF = jnp.bfloat16
F32 = jnp.float32


def normalize(values, axis_at):
    average = jnp.mean(values, axis=axis_at, keepdims=True)
    centred = values - average
    variance = jnp.mean(centred * centred, axis=axis_at, keepdims=True)
    return centred * lax.rsqrt(variance + 1e-05)


def gather_grp(value, axis_at):
    size = lax.axis_size("grp")
    far = lax.ppermute(value, "grp", [(i, i ^ 2) for i in range(size)])
    both = jnp.concatenate([value, far], axis=axis_at)
    near = lax.ppermute(both, "grp", [(i, i ^ 1) for i in range(size)])
    return jnp.concatenate([both, near], axis=axis_at)


def attention_kernel(
    heads,
    head_size,
    row_ref,
    qt_ref,
    dmt_ref,
    gt_ref,
    kv0_ref,
    kv1_ref,
    kv2_ref,
    kv3_ref,
    bias_ref,
    gated_ref,
    grad_ref,
    k_s,
    v_s,
    qbd,
    dbd,
    st,
    dpt,
    pt,
    gacc,
):
    samples, width, rows = qt_ref.shape
    row_count = 4
    keys = rows * row_count
    scale = 1.0 / math.sqrt(head_size)
    row_at = row_ref[0]
    qbd[...] = jnp.zeros_like(qbd)
    dbd[...] = jnp.zeros_like(dbd)
    chunk = 64
    groups = chunk // 8

    def one_sample(s, unused):
        for step, ref in enumerate((kv0_ref, kv1_ref, kv2_ref, kv3_ref)):
            block = lax.rem(row_at + row_count - step, row_count)
            at = pl.multiple_of(block * rows, rows)
            k_s[pl.ds(at, rows), :] = ref[s, :, 0:width]
            v_s[pl.ds(at, rows), :] = ref[s, :, width : 2 * width]
        for h in range(heads):
            e0, i0 = h * head_size, h * rows
            qbd[e0 : e0 + head_size, i0 : i0 + rows] = qt_ref[s, e0 : e0 + head_size, :]
            dbd[e0 : e0 + head_size, i0 : i0 + rows] = dmt_ref[s, e0 : e0 + head_size, :]
        st[...] = jnp.dot(k_s[...], qbd[...], preferred_element_type=F32)
        dpt[...] = jnp.dot(v_s[...], dbd[...], preferred_element_type=F32)
        for h in range(heads):
            e0, i0 = h * head_size, h * rows
            lanes = slice(i0, i0 + rows)
            top = jnp.full((8, rows), -jnp.inf, F32)
            for b in range(keys // chunk):
                part = slice(b * chunk, (b + 1) * chunk)
                bias = bias_ref[b * groups : (b + 1) * groups, h, :, :].reshape(chunk, rows)
                x = st[part, lanes] * scale + bias
                st[part, lanes] = x
                top = jnp.maximum(top, jnp.max(x.reshape(groups, 8, rows), axis=0))
            peak = jnp.max(top, axis=0, keepdims=True)
            total = jnp.zeros((8, rows), F32)
            dots = jnp.zeros((8, rows), F32)
            for b in range(keys // chunk):
                part = slice(b * chunk, (b + 1) * chunk)
                w = jnp.exp(st[part, lanes] - peak)
                st[part, lanes] = w
                total = total + jnp.sum(w.reshape(groups, 8, rows), axis=0)
                dots = dots + jnp.sum((w * dpt[part, lanes]).reshape(groups, 8, rows), axis=0)
            inverse = 1.0 / jnp.sum(total, axis=0, keepdims=True)
            inner = jnp.sum(dots, axis=0, keepdims=True) * inverse
            for b in range(keys // chunk):
                part = slice(b * chunk, (b + 1) * chunk)
                p = st[part, lanes] * inverse
                pt[part, lanes] = p.astype(BF)
                d = p * (dpt[part, lanes] - inner)

                @pl.when(s == 0)
                def _():
                    gacc[h, part, :] = d

                @pl.when(s > 0)
                def _():
                    gacc[h, part, :] = gacc[h, part, :] + d

            mixed = lax.dot_general(
                v_s[...],
                pt[:, lanes],
                (((0,), (0,)), ((), ())),
                preferred_element_type=F32,
            )
            gated_ref[s, e0 : e0 + head_size, :] = (
                mixed[e0 : e0 + head_size, :] * gt_ref[s, e0 : e0 + head_size, :]
            ).astype(BF)
        return unused

    lax.fori_loop(0, samples, one_sample, 0)
    parts, _, width_j, _ = grad_ref.shape
    for h in range(heads):
        for c in range(parts):
            grad_ref[c, h, :, :] = gacc[h, c * width_j : (c + 1) * width_j, :].astype(BF)


def on_device(
    pair_rep,
    residue_index,
    chain_index,
    token_mask,
    relpos_table,
    proj_in,
    out_proj,
    bias_weight,
    single_rep,
    w_qkvg,
    w_out,
    cotangent,
):
    tok_rows, col_width, channels = pair_rep.shape
    col_count = lax.axis_size("col")
    grp_count = lax.axis_size("grp")
    row_count = lax.axis_size("row")
    row_at = lax.axis_index("row")
    grp_at = lax.axis_index("grp")
    col_at = lax.axis_index("col")
    samples = single_rep.shape[0]
    head_width = w_out.shape[0]
    all_heads = bias_weight.shape[1]
    heads = all_heads // grp_count
    head_size = head_width // heads
    row_start = row_at * tok_rows
    col_start = (grp_at * col_count + col_at) * col_width
    table = jnp.stack([residue_index, chain_index, token_mask])
    of_rows = lax.dynamic_slice_in_dim(table, row_start, tok_rows, 1)
    of_cols = lax.dynamic_slice_in_dim(table, col_start, col_width, 1)
    mask_rows, mask_cols = of_rows[2], of_cols[2]

    normed_x = normalize(single_rep.astype(F32), 2).astype(BF)
    key_value = jnp.einsum(
        "srd,tde->srte", normed_x, w_qkvg[1:3], preferred_element_type=F32
    )
    keep_rows = (mask_rows == 1)[None, :, None, None]
    is_value = (jnp.arange(2) == 1)[None, None, :, None]
    key_value = jnp.where(keep_rows | is_value, key_value, 0.0).astype(BF)
    key_value = key_value.reshape(samples, tok_rows, 2 * head_width)
    moved = [
        lax.ppermute(
            key_value, "row", [(i, (i + step) % row_count) for i in range(row_count)]
        )
        for step in range(1, row_count)
    ]

    pair_tile = pair_rep.transpose(1, 0, 2).astype(F32)
    offsets = jnp.clip(of_rows[0][None, :] - of_cols[0][:, None], -32, 32) + 32
    bin_ids = jnp.where(of_rows[1][None, :] == of_cols[1][:, None], offsets, 65)
    onehot = (
        bin_ids[:, :, None] == jnp.arange(relpos_table.shape[0], dtype=jnp.int32)[None, None, :]
    ).astype(BF)
    pair_in = pair_tile + jnp.einsum(
        "jib,bc->jic", onehot, relpos_table, preferred_element_type=F32
    )
    normed = normalize(pair_in, 2).astype(BF)
    projected = jnp.einsum(
        "jic,ce->eji", normed, proj_in[:, : 4 * channels], preferred_element_type=F32
    )
    pair_mask = (mask_cols[:, None] * mask_rows[None, :]).astype(F32)[None]
    left_in = (
        jax.nn.sigmoid(projected[2 * channels : 3 * channels]) * projected[:channels] * pair_mask
    ).astype(BF)
    right_in = (
        jax.nn.sigmoid(projected[3 * channels :]) * projected[channels : 2 * channels] * pair_mask
    ).astype(BF)
    half = col_width // 2
    everyone = ("row", "col", "grp")
    count = row_count * col_count * grp_count
    send = jnp.stack(
        [
            left_in.reshape(channels, 2, half, tok_rows),
            right_in.reshape(channels, 2, half, tok_rows),
        ],
        axis=2,
    ).reshape(count, 2 * half, tok_rows)
    got = lax.all_to_all(send, everyone, 0, 0, tiled=True)
    got = got.reshape(row_count, col_count, grp_count, 2, half, tok_rows)
    left_own, right_own = got[:, :, :, 0], got[:, :, :, 1]
    left_other = lax.ppermute(left_own, "grp", [(i, i ^ 1) for i in range(grp_count)])
    first = (grp_at % 2) == 0
    left_all = (
        jnp.stack(
            [jnp.where(first, left_own, left_other), jnp.where(first, left_other, left_own)],
            axis=3,
        )
        .transpose(0, 2, 1, 3, 4, 5)
        .reshape(row_count, grp_count, tok_rows, tok_rows)
    )
    right_all = right_own.reshape(row_count, count * half // row_count, tok_rows)
    triangle = jnp.einsum("rgik,rjk->gji", left_all, right_all, preferred_element_type=F32)
    back = triangle.astype(BF).reshape(count, half, tok_rows)
    tri_local = lax.all_to_all(back, everyone, 0, 0, tiled=True)
    tri_local = tri_local.reshape(channels, col_width, tok_rows)
    out_normed = normalize(tri_local.astype(F32), 0).astype(BF)
    gate_out = jax.nn.sigmoid(
        jnp.einsum("jic,cd->jid", normed, proj_in[:, 4 * channels :], preferred_element_type=F32)
    )
    update = jnp.einsum("cji,cd->jid", out_normed, out_proj, preferred_element_type=F32)
    pair_new = pair_in + gate_out * update
    pair_out = pair_new.astype(BF).transpose(1, 0, 2)
    bias_local = jnp.einsum(
        "jic,ch->hji", normalize(pair_new, 2), bias_weight, precision=lax.Precision.HIGHEST
    )
    bias_local = jnp.where((mask_cols == 1)[None, :, None], bias_local, -1000000000.0)
    copies = jnp.broadcast_to(
        bias_local.reshape(grp_count, 1, heads, col_width, tok_rows),
        (grp_count, col_count, heads, col_width, tok_rows),
    ).reshape(grp_count * col_count, heads, col_width, tok_rows)
    bias_all = lax.all_to_all(copies, ("grp", "col"), 0, 0, tiled=True)

    query_t = jnp.einsum("srd,de->ser", normed_x, w_qkvg[0], preferred_element_type=F32).astype(BF)
    gate_t = jax.nn.sigmoid(
        jnp.einsum("srd,de->ser", normed_x, w_qkvg[3], preferred_element_type=F32)
    )
    back_t = jnp.einsum("srd,ed->ser", cotangent, w_out, preferred_element_type=F32)
    d_mixed_t = (back_t * gate_t).astype(BF)
    weights = gather_grp(w_out, 0)
    keys = row_count * tok_rows
    vmem = pl.BlockSpec(memory_space=pltpu.VMEM)
    gated_t, grads = pl.pallas_call(
        lambda *refs: attention_kernel(heads, head_size, *refs),
        out_shape=(
            jax.ShapeDtypeStruct((samples, head_width, tok_rows), BF),
            jax.ShapeDtypeStruct((col_count, heads, keys // col_count, tok_rows), BF),
        ),
        in_specs=[pl.BlockSpec(memory_space=pltpu.SMEM)] + [vmem] * 8,
        out_specs=(vmem, vmem),
        scratch_shapes=[
            pltpu.VMEM((keys, head_width), BF),
            pltpu.VMEM((keys, head_width), BF),
            pltpu.VMEM((head_width, heads * tok_rows), BF),
            pltpu.VMEM((head_width, heads * tok_rows), BF),
            pltpu.VMEM((keys, heads * tok_rows), F32),
            pltpu.VMEM((keys, heads * tok_rows), F32),
            pltpu.VMEM((keys, heads * tok_rows), BF),
            pltpu.VMEM((heads, keys, tok_rows), F32),
        ],
        name="attention",
    )(
        row_at.astype(jnp.int32).reshape(1),
        query_t,
        d_mixed_t,
        gate_t,
        key_value,
        *moved,
        bias_all,
    )
    gated_parts = gather_grp(gated_t, 1)
    grad_parts = lax.all_to_all(grads, "col", 0, 0, tiled=True)
    grad_sum = jnp.sum(grad_parts.astype(F32), axis=0)
    bias_grad = grad_sum.transpose(0, 2, 1)
    mixed_out = jnp.einsum(
        "ser,ed->srd",
        gated_parts,
        weights,
        preferred_element_type=F32,
    )
    single_out = (single_rep.astype(F32) + mixed_out).astype(BF)
    return (pair_out, single_out, bias_grad)


def solution(mesh):
    placed = (
        P("row", ("grp", "col"), None),
        P(),
        P(),
        P(),
        P(),
        P(),
        P(),
        P(),
        P("col", "row", None),
        P(None, None, "grp"),
        P("grp", None),
        P("col", "row", None),
    )

    return jax.shard_map(
        on_device,
        mesh=mesh,
        in_specs=placed,
        out_specs=(P("row", ("grp", "col"), None), P("col", "row", None), P("grp", "row", "col")),
        check_vma=False,
    )
```

profile of v0, /device:TPU:2, one launch (start us, length us, event | category | flops | bytes accessed | tf_op | source)
XLA Modules:
  0.0 158.7 jit_solution(7022550456142454303)
XLA Ops:
  0.7 0.8 pad_add_fusion
  1.6 1.1 copy.27
  2.8 1.0 fusion.72
  5.5 34.2 %all_to_all.20 = bf16[256,8,128]{2,1,0:T(8,128)(2,1)S(1)} all-to-all(bf16[256,8,128]{2,1,0:T(8,128)(2,1)S(1)} %bitcast.146), channel_id=1, replica_groups=mesh['grp'=4,'row'=4,'col'=16] {'row','col','grp'}, dimensions={0} | all-to-all | bytes 1048576 | tf_op jit(solution)/shard_map/all_to_all | solution.py:205
  40.3 1.3 collective-permute-done
  42.4 1.0 fusion.7
  43.4 6.9 %all-to-all-start.1 = ((bf16[256,4,128]{2,1,0:T(4,128)(2,1)}), bf16[256,4,128]{2,1,0:T(4,128)(2,1)S(1)}, u32[]{:S(2)}, u32[]{:S(2)}) async-start(bf16[256,4,128]{2,1,0:T(4,128)(2,1)} %bitcast.29), calls=%async_computation.1 | async-start | bytes 524288 | tf_op jit(solution)/shard_map/all_to_all | solution.py:221
  50.9 14.5 %all-to-all-done.1 = bf16[256,4,128]{2,1,0:T(4,128)(2,1)S(1)} async-done(((bf16[256,4,128]{2,1,0:T(4,128)(2,1)}), bf16[256,4,128]{2,1,0:T(4,128)(2,1)S(1)}, u32[]{:S(2)}, u32[]{:S(2)}) %all-to-all-start.1) | async-done | bytes 262176 | tf_op jit(solution)/shard_map/all_to_all | solution.py:221
  67.2 1.1 broadcast_in_dim.55
  68.3 5.6 %all-to-all-start.2 = ((f32[64,4,8,128]{3,2,1,0:T(8,128)}), f32[64,4,8,128]{3,2,1,0:T(8,128)S(1)}, u32[]{:S(2)}, u32[]{:S(2)}) async-start(f32[64,4,8,128]{3,2,1,0:T(8,128)} %bitcast.50), calls=%async_computation.2 | async-start | bytes 2097152 | tf_op jit(solution)/shard_map/all_to_all | solution.py:238
  74.4 2.5 %fusion.6 = bf16[3,128,2,192]{1,3,2,0:T(8,128)(2,1)} fusion(bf16[4,768,192]{1,2,0:T(8,128)(2,1)} %param.21, bf16[3,128,768]{2,1,0:T(8,128)(2,1)S(1)} %copy-done.2, f32[3,128]{1,0:T(4,128)S(1)} %add_rsqrt_fusion.3, f32[3,128]{1,0:T(4,128)S(1)} %broadcast_multiply_fusion.3, pred[128,2]{0,1:T(4,128)(4,1)S(1)} %broadcast_or_fusion), kind=kOutput, calls=%fused_computation.14 | convolution fusion | flops 227966976 | bytes 1477888 | tf_op jit(solution)/shard_map/srd,tde->srte/dot_general | solution.py:161
  76.8 1.2 copy.41.refs_4_
  78.0 0.7 collective-permute-start.1
  78.7 2.7 %collective-permute-start.2 = (bf16[3,128,384]{2,1,0:T(8,128)(2,1)S(1)}, bf16[3,128,384]{2,1,0:T(8,128)(2,1)S(1)}, u32[]{:S(2)}, u32[]{:S(2)}) collective-permute-start(bf16[3,128,384]{2,1,0:T(8,128)(2,1)S(1)} %copy.41.refs_4_), channel_id=1, source_target_pairs={{0,32},{16,48},{32,0},{48,16},{1,33},{17,49},{33,1},{49,17},{2,34}... | collective-permute-start | bytes 884744 | tf_op jit(solution)/shard_map/ppermute | solution.py:169
  81.4 2.0 %collective-permute-start.3 = (bf16[3,128,384]{2,1,0:T(8,128)(2,1)S(1)}, bf16[3,128,384]{2,1,0:T(8,128)(2,1)}, u32[]{:S(2)}, u32[]{:S(2)}) collective-permute-start(bf16[3,128,384]{2,1,0:T(8,128)(2,1)S(1)} %copy.41.refs_4_), channel_id=1, source_target_pairs={{0,48},{16,0},{32,16},{48,32},{1,49},{17,1},{33,17},{49,33},{2,50}... | collective-permute-start | bytes 884744 | tf_op jit(solution)/shard_map/ppermute | solution.py:169
  83.4 1.6 %collective-permute-start.6 = (bf16[192,768]{1,0:T(8,128)(2,1)S(1)}, bf16[192,768]{1,0:T(8,128)(2,1)S(1)}, u32[]{:S(2)}, u32[]{:S(2)}) collective-permute-start(bf16[192,768]{1,0:T(8,128)(2,1)S(1)} %copy-done.5), channel_id=1, source_target_pairs={{0,128},{64,192},{128,0},{192,64},{1,129},{65,193},{129,1},{193,65... | collective-permute-start | bytes 884744 | tf_op jit(solution)/shard_map/ppermute | solution.py:23
  85.0 1.5 fusion.18.refs_3_
  86.5 1.0 fusion.19.refs_2_
  87.5 31.9 %collective-permute-done.6 = bf16[192,768]{1,0:T(8,128)(2,1)S(1)} collective-permute-done((bf16[192,768]{1,0:T(8,128)(2,1)S(1)}, bf16[192,768]{1,0:T(8,128)(2,1)S(1)}, u32[]{:S(2)}, u32[]{:S(2)}) %collective-permute-start.6) | collective-permute-done | bytes 294944 | tf_op jit(solution)/shard_map/ppermute | solution.py:23
  119.4 0.9 pad_maximum_fusion
  120.3 2.1 %fusion.20.refs_1_ = bf16[3,192,128]{2,1,0:T(8,128)(2,1)} fusion(bf16[3,128,768]{2,1,0:T(8,128)(2,1)S(1)} %copy-done.2, f32[3,128]{1,0:T(4,128)S(1)} %add_rsqrt_fusion.3, f32[3,128]{1,0:T(4,128)S(1)} %broadcast_multiply_fusion.3, bf16[4,768,192]{1,2,0:T(8,128)(2,1)} %param.21), kind=kOutput, calls=%fused_computation.32 | convolution fusion | flops 114499584 | bytes 1035264 | tf_op jit(solution)/shard_map/srd,de->ser/dot_general | solution.py:240
  122.4 0.7 copy-done.6
  123.1 0.7 copy-done.7
  123.8 1.0 copy-done.1
  124.8 8.5 %attention.1 = (bf16[3,192,128]{2,1,0:T(8,128)(2,1)}, bf16[16,4,32,128]{3,2,1,0:T(8,128)(2,1)}) custom-call(s32[1]{0:T(128)} %bitcast.34.refs_0_, bf16[3,192,128]{2,1,0:T(8,128)(2,1)} %fusion.20.refs_1_, bf16[3,192,128]{2,1,0:T(8,128)(2,1)} %fusion.19.refs_2_, f32[3,192,128]{2,1,0:T(8,128)} %copy-done.4, bf16[3,128,384]{2,1,0:T(8,128)(2,1)} %copy-done.3, ...), custom_call_target="tpu_custom_call" | custom-call | tf_op jit(solution)/shard_map/attention/pallas_call | solution.py:249
  133.7 6.1 %collective-permute-done.4 = bf16[3,192,128]{2,1,0:T(8,128)(2,1)S(1)} collective-permute-done((bf16[3,192,128]{2,1,0:T(8,128)(2,1)}, bf16[3,192,128]{2,1,0:T(8,128)(2,1)S(1)}, u32[]{:S(2)}, u32[]{:S(2)}) %collective-permute-start.4) | collective-permute-done | bytes 147488 | tf_op jit(solution)/shard_map/ppermute | solution.py:23
  139.8 0.9 pad_maximum_fusion.2
  140.9 7.3 %all-to-all-start.3 = ((bf16[16,4,32,128]{3,2,1,0:T(8,128)(2,1)}), bf16[16,4,32,128]{3,2,1,0:T(8,128)(2,1)S(1)}, u32[]{:S(2)}, u32[]{:S(2)}) async-start(bf16[16,4,32,128]{3,2,1,0:T(8,128)(2,1)} %get-tuple-element.6), calls=%async_computation.3 | async-start | bytes 1048576 | tf_op jit(solution)/shard_map/all_to_all | solution.py:278
  148.1 0.9 copy.43
  149.0 2.6 %fusion.2 = bf16[3,128,768]{2,1,0:T(8,128)(2,1)} fusion(bf16[3,128,768]{2,1,0:T(8,128)(2,1)S(1)} %copy-done.2, bf16[384,768]{1,0:T(8,128)(2,1)} %collective-permute-done.7, bf16[192,768]{1,0:T(8,128)(2,1)S(1)} %copy-done.9, bf16[192,768]{1,0:T(8,128)(2,1)S(1)} %copy-done.5, bf16[3,384,128]{2,1,0:T(8,128)(2,1)S(1)} %collective-permute-done.5, ...), kind=kOutput, calls=%fused_computation.6 | convolution fusion | flops 459177984 | bytes 2949120 | tf_op jit(solution)/shard_map/ser,ed->srd/dot_general | solution.py:281
  151.6 6.4 %all-to-all-done.3 = bf16[16,4,32,128]{3,2,1,0:T(8,128)(2,1)S(1)} async-done(((bf16[16,4,32,128]{3,2,1,0:T(8,128)(2,1)}), bf16[16,4,32,128]{3,2,1,0:T(8,128)(2,1)S(1)}, u32[]{:S(2)}, u32[]{:S(2)}) %all-to-all-start.3) | async-done | bytes 524320 | tf_op jit(solution)/shard_map/all_to_all | solution.py:278
  158.0 0.7 convert_reduce_fusion.1
  (73 shorter events, 6.4 us)
Async XLA Ops:
  0.6 85.8 %copy-start = (bf16[3,128,768]{2,1,0:T(8,128)(2,1)S(1)}, bf16[3,128,768]{2,1,0:T(8,128)(2,1)}, u32[]{:S(2)}) copy-start(bf16[3,128,768]{2,1,0:T(8,128)(2,1)} %param.23) | copy-start | bytes 1769476
  0.6 3.3 %copy-start.11 = (bf16[128,640]{1,0:T(8,128)(2,1)S(1)}, bf16[128,640]{1,0:T(8,128)(2,1)}, u32[]{:S(2)}) copy-start(bf16[128,640]{1,0:T(8,128)(2,1)} %param.17) | copy-start | bytes 491524
  39.9 1.6 %collective-permute-start = (bf16[4,16,4,4,128]{4,3,2,1,0:T(4,128)(2,1)S(1)}, bf16[4,16,4,4,128]{4,3,2,1,0:T(4,128)(2,1)S(1)}, u32[]{:S(2)}, u32[]{:S(2)}) collective-permute-start(bf16[4,16,4,4,128]{4,3,2,1,0:T(4,128)(2,1)S(1)} %get-tuple-element.19), channel_id=1, source_target_pairs={{0,64},{64,0},{128,192},{192,128},{1,65},{65,1},{129,193},{193,129... | collective-permute-start | bytes 786440 | tf_op jit(solution)/shard_map/ppermute | solution.py:208
  42.1 8.2 %copy-start.2 = (bf16[3,128,768]{2,1,0:T(8,128)(2,1)S(1)}, bf16[3,128,768]{2,1,0:T(8,128)(2,1)}, u32[]{:S(2)}) copy-start(bf16[3,128,768]{2,1,0:T(8,128)(2,1)} %param.20) | copy-start | bytes 1769476
  43.4 22.0 %all-to-all-start.1 = ((bf16[256,4,128]{2,1,0:T(4,128)(2,1)}), bf16[256,4,128]{2,1,0:T(4,128)(2,1)S(1)}, u32[]{:S(2)}, u32[]{:S(2)}) async-start(bf16[256,4,128]{2,1,0:T(4,128)(2,1)} %bitcast.29), calls=%async_computation.1 | async-start | bytes 524288 | tf_op jit(solution)/shard_map/all_to_all | solution.py:221
  50.5 15.3 %copy-start.12 = (bf16[128,128]{1,0:T(8,128)(2,1)S(1)}, bf16[128,128]{1,0:T(8,128)(2,1)}, u32[]{:S(2)}) copy-start(bf16[128,128]{1,0:T(8,128)(2,1)} %param.18) | copy-start | bytes 98308
  66.1 0.7 copy-start.13
  68.3 55.5 %all-to-all-start.2 = ((f32[64,4,8,128]{3,2,1,0:T(8,128)}), f32[64,4,8,128]{3,2,1,0:T(8,128)S(1)}, u32[]{:S(2)}, u32[]{:S(2)}) async-start(f32[64,4,8,128]{3,2,1,0:T(8,128)} %bitcast.50), calls=%async_computation.2 | async-start | bytes 2097152 | tf_op jit(solution)/shard_map/all_to_all | solution.py:238
  74.3 9.0 %copy-start.5 = (bf16[192,768]{1,0:T(8,128)(2,1)S(1)}, bf16[192,768]{1,0:T(8,128)(2,1)}, u32[]{:S(2)}) copy-start(bf16[192,768]{1,0:T(8,128)(2,1)} %param.22) | copy-start | bytes 884740
  78.0 8.4 %copy-start.3 = (bf16[3,128,384]{2,1,0:T(8,128)(2,1)}, bf16[3,128,384]{2,1,0:T(8,128)(2,1)S(1)}, u32[]{:S(2)}) copy-start(bf16[3,128,384]{2,1,0:T(8,128)(2,1)S(1)} %copy.41.refs_4_) | copy-start | bytes 884740
  78.0 44.4 %collective-permute-start.1 = (bf16[3,128,384]{2,1,0:T(8,128)(2,1)S(1)}, bf16[3,128,384]{2,1,0:T(8,128)(2,1)S(1)}, u32[]{:S(2)}, u32[]{:S(2)}) collective-permute-start(bf16[3,128,384]{2,1,0:T(8,128)(2,1)S(1)} %copy.41.refs_4_), channel_id=1, source_target_pairs={{0,16},{16,32},{32,48},{48,0},{1,17},{17,33},{33,49},{49,1},{2,18}... | collective-permute-start | bytes 884744 | tf_op jit(solution)/shard_map/ppermute | solution.py:169
  78.7 43.7 %collective-permute-start.2 = (bf16[3,128,384]{2,1,0:T(8,128)(2,1)S(1)}, bf16[3,128,384]{2,1,0:T(8,128)(2,1)S(1)}, u32[]{:S(2)}, u32[]{:S(2)}) collective-permute-start(bf16[3,128,384]{2,1,0:T(8,128)(2,1)S(1)} %copy.41.refs_4_), channel_id=1, source_target_pairs={{0,32},{16,48},{32,0},{48,16},{1,33},{17,49},{33,1},{49,17},{2,34}... | collective-permute-start | bytes 884744 | tf_op jit(solution)/shard_map/ppermute | solution.py:169
  81.4 42.4 %collective-permute-start.3 = (bf16[3,128,384]{2,1,0:T(8,128)(2,1)S(1)}, bf16[3,128,384]{2,1,0:T(8,128)(2,1)}, u32[]{:S(2)}, u32[]{:S(2)}) collective-permute-start(bf16[3,128,384]{2,1,0:T(8,128)(2,1)S(1)} %copy.41.refs_4_), channel_id=1, source_target_pairs={{0,48},{16,0},{32,16},{48,32},{1,49},{17,1},{33,17},{49,33},{2,50}... | collective-permute-start | bytes 884744 | tf_op jit(solution)/shard_map/ppermute | solution.py:169
  83.4 36.0 %collective-permute-start.6 = (bf16[192,768]{1,0:T(8,128)(2,1)S(1)}, bf16[192,768]{1,0:T(8,128)(2,1)S(1)}, u32[]{:S(2)}, u32[]{:S(2)}) collective-permute-start(bf16[192,768]{1,0:T(8,128)(2,1)S(1)} %copy-done.5), channel_id=1, source_target_pairs={{0,128},{64,192},{128,0},{192,64},{1,129},{65,193},{129,1},{193,65... | collective-permute-start | bytes 884744 | tf_op jit(solution)/shard_map/ppermute | solution.py:23
  86.4 33.8 %copy-start.4 = (f32[3,192,128]{2,1,0:T(8,128)}, f32[3,192,128]{2,1,0:T(8,128)S(1)}, u32[]{:S(2)}) copy-start(f32[3,192,128]{2,1,0:T(8,128)S(1)} %fusion.18.refs_3_) | copy-start | bytes 884740
  119.4 3.0 %copy-start.8 = (bf16[192,768]{1,0:T(8,128)(2,1)}, bf16[192,768]{1,0:T(8,128)(2,1)S(1)}, u32[]{:S(2)}) copy-start(bf16[192,768]{1,0:T(8,128)(2,1)S(1)} %collective-permute-done.6) | copy-start | bytes 884740
  120.3 28.7 %collective-permute-start.7 = (bf16[384,768]{1,0:T(8,128)(2,1)}, bf16[384,768]{1,0:T(8,128)(2,1)}, u32[]{:S(2)}, u32[]{:S(2)}) collective-permute-start(bf16[384,768]{1,0:T(8,128)(2,1)} %pad_maximum_fusion), channel_id=1, source_target_pairs={{0,64},{64,0},{128,192},{192,128},{1,65},{65,1},{129,193},{193,129... | collective-permute-start | bytes 1769480 | tf_op jit(solution)/shard_map/ppermute | solution.py:25
  122.4 0.7 copy-start.6
  123.1 0.7 copy-start.7
  123.8 1.0 copy-start.1
  133.3 15.7 %copy-start.9 = (bf16[192,768]{1,0:T(8,128)(2,1)S(1)}, bf16[192,768]{1,0:T(8,128)(2,1)}, u32[]{:S(2)}) copy-start(bf16[192,768]{1,0:T(8,128)(2,1)} %copy-done.8) | copy-start | bytes 884740
  133.3 15.7 %copy-start.10 = (bf16[3,192,128]{2,1,0:T(8,128)(2,1)S(1)}, bf16[3,192,128]{2,1,0:T(8,128)(2,1)}, u32[]{:S(2)}) copy-start(bf16[3,192,128]{2,1,0:T(8,128)(2,1)} %get-tuple-element.5) | copy-start | bytes 442372
  133.3 6.5 %collective-permute-start.4 = (bf16[3,192,128]{2,1,0:T(8,128)(2,1)}, bf16[3,192,128]{2,1,0:T(8,128)(2,1)S(1)}, u32[]{:S(2)}, u32[]{:S(2)}) collective-permute-start(bf16[3,192,128]{2,1,0:T(8,128)(2,1)} %get-tuple-element.5), channel_id=1, source_target_pairs={{0,128},{64,192},{128,0},{192,64},{1,129},{65,193},{129,1},{193,65... | collective-permute-start | bytes 442376 | tf_op jit(solution)/shard_map/ppermute | solution.py:23
  140.8 8.3 %collective-permute-start.5 = (bf16[3,384,128]{2,1,0:T(8,128)(2,1)S(1)}, bf16[3,384,128]{2,1,0:T(8,128)(2,1)S(1)}, u32[]{:S(2)}, u32[]{:S(2)}) collective-permute-start(bf16[3,384,128]{2,1,0:T(8,128)(2,1)S(1)} %pad_maximum_fusion.2), channel_id=1, source_target_pairs={{0,64},{64,0},{128,192},{192,128},{1,65},{65,1},{129,193},{193,129... | collective-permute-start | bytes 884744 | tf_op jit(solution)/shard_map/ppermute | solution.py:25
  140.9 17.2 %all-to-all-start.3 = ((bf16[16,4,32,128]{3,2,1,0:T(8,128)(2,1)}), bf16[16,4,32,128]{3,2,1,0:T(8,128)(2,1)S(1)}, u32[]{:S(2)}, u32[]{:S(2)}) async-start(bf16[16,4,32,128]{3,2,1,0:T(8,128)(2,1)} %get-tuple-element.6), calls=%async_computation.3 | async-start | bytes 1048576 | tf_op jit(solution)/shard_map/all_to_all | solution.py:278
where the time goes:
time: 160 us; the launch traced here: 159 us
  waiting for transfers between devices  60.3 us (38%)
  blocking collectives  34.2 us (21%)
  starting transfers between devices  27.6 us (17%)
  matrix products  13.1 us (8%)
  Pallas kernels  8.53 us (5%)
  local copies, waits for them, and re-layouts  8.15 us (5%)
  other arithmetic  5.9 us (4%)
    ppermute x2, waiting for transfers between devices, gather_grp(): far = lax.ppermute(value, 'grp', [(i, i ^ 2) for i in range(size)])  38 us
    all_to_all x1, blocking collectives, on_device(): got = lax.all_to_all(send, everyone, 0, 0, tiled=True)  34.2 us
    all_to_all x1, waiting for transfers between devices, on_device(): tri_local = lax.all_to_all(back, everyone, 0, 0, tiled=True)  14.5 us
    pallas_call x1, Pallas kernels, on_device(): pl.pallas_call(lambda *refs: attention_kernel(heads, head_size, *refs), o...  8.53 us
    all_to_all x1, starting transfers between devices, on_device(): grad_parts = lax.all_to_all(grads, 'col', 0, 0, tiled=True)  7.27 us
    all_to_all x1, starting transfers between devices, on_device(): tri_local = lax.all_to_all(back, everyone, 0, 0, tiled=True)  6.91 us
    all_to_all x1, waiting for transfers between devices, on_device(): grad_parts = lax.all_to_all(grads, 'col', 0, 0, tiled=True)  6.43 us
    all_to_all x1, starting transfers between devices, on_device(): bias_all = lax.all_to_all(copies, ('grp', 'col'), 0, 0, tiled=True)  5.58 us
  transfers between devices with their start and end apart: 11, of which 5 were waited for; matrix products, arithmetic and copies ran while one was open for 9% of the time, Pallas kernels for 5%

commit v1 on v0

--- a/solution.py
+++ b/solution.py
@@ -5,6 +5,7 @@
 from jax import lax
 from jax.experimental import pallas as pl
 from jax.experimental.pallas import tpu as pltpu
+from jax.sharding import Mesh
 from jax.sharding import PartitionSpec as P
 
 BF = jnp.bfloat16
@@ -18,11 +19,13 @@
     return centred * lax.rsqrt(variance + 1e-05)
 
 
+SWAP = [(0, 1), (1, 0)]
+
+
 def gather_grp(value, axis_at):
-    size = lax.axis_size("grp")
-    far = lax.ppermute(value, "grp", [(i, i ^ 2) for i in range(size)])
+    far = lax.ppermute(value, "near", SWAP)
     both = jnp.concatenate([value, far], axis=axis_at)
-    near = lax.ppermute(both, "grp", [(i, i ^ 1) for i in range(size)])
+    near = lax.ppermute(both, "core", SWAP)
     return jnp.concatenate([both, near], axis=axis_at)
 
 
@@ -33,10 +36,11 @@
     qt_ref,
     dmt_ref,
     gt_ref,
-    kv0_ref,
-    kv1_ref,
-    kv2_ref,
-    kv3_ref,
+    own_ref,
+    last_ref,
+    next_ref,
+    top_ref,
+    low_ref,
     bias_ref,
     gated_ref,
     grad_ref,
@@ -60,11 +64,19 @@
     groups = chunk // 8
 
     def one_sample(s, unused):
-        for step, ref in enumerate((kv0_ref, kv1_ref, kv2_ref, kv3_ref)):
+        for step, halves in enumerate(
+            (
+                (own_ref.at[0], own_ref.at[1]),
+                (last_ref.at[0], last_ref.at[1]),
+                (top_ref, low_ref),
+                (next_ref.at[0], next_ref.at[1]),
+            )
+        ):
             block = lax.rem(row_at + row_count - step, row_count)
-            at = pl.multiple_of(block * rows, rows)
-            k_s[pl.ds(at, rows), :] = ref[s, :, 0:width]
-            v_s[pl.ds(at, rows), :] = ref[s, :, width : 2 * width]
+            for n, ref in enumerate(halves):
+                at = pl.multiple_of(block * rows + n * (rows // 2), rows // 2)
+                k_s[pl.ds(at, rows // 2), :] = ref[s, :, 0:width]
+                v_s[pl.ds(at, rows // 2), :] = ref[s, :, width : 2 * width]
         for h in range(heads):
             e0, i0 = h * head_size, h * rows
             qbd[e0 : e0 + head_size, i0 : i0 + rows] = qt_ref[s, e0 : e0 + head_size, :]
@@ -140,10 +152,13 @@
 ):
     tok_rows, col_width, channels = pair_rep.shape
     col_count = lax.axis_size("col")
-    grp_count = lax.axis_size("grp")
+    near_count = lax.axis_size("near")
+    core_count = lax.axis_size("core")
+    grp_count = near_count * core_count
     row_count = lax.axis_size("row")
     row_at = lax.axis_index("row")
-    grp_at = lax.axis_index("grp")
+    core_at = lax.axis_index("core")
+    grp_at = lax.axis_index("near") * core_count + core_at
     col_at = lax.axis_index("col")
     samples = single_rep.shape[0]
     head_width = w_out.shape[0]
@@ -164,13 +179,14 @@
     keep_rows = (mask_rows == 1)[None, :, None, None]
     is_value = (jnp.arange(2) == 1)[None, None, :, None]
     key_value = jnp.where(keep_rows | is_value, key_value, 0.0).astype(BF)
-    key_value = key_value.reshape(samples, tok_rows, 2 * head_width)
-    moved = [
-        lax.ppermute(
-            key_value, "row", [(i, (i + step) % row_count) for i in range(row_count)]
-        )
-        for step in range(1, row_count)
-    ]
+    key_value = key_value.reshape(samples, 2, tok_rows // 2, 2 * head_width).transpose(1, 0, 2, 3)
+    onward = [(i, (i + 1) % row_count) for i in range(row_count)]
+    backward = [(i, (i + row_count - 1) % row_count) for i in range(row_count)]
+    from_last = lax.ppermute(key_value, "row", onward)
+    from_next = lax.ppermute(key_value, "row", backward)
+    last_half, next_half = from_last[0], from_next[1]
+    far_top = lax.ppermute(last_half, "row", onward)
+    far_low = lax.ppermute(next_half, "row", backward)
 
     pair_tile = pair_rep.transpose(1, 0, 2).astype(F32)
     offsets = jnp.clip(of_rows[0][None, :] - of_cols[0][:, None], -32, 32) + 32
@@ -192,33 +208,26 @@
     right_in = (
         jax.nn.sigmoid(projected[3 * channels :]) * projected[channels : 2 * channels] * pair_mask
     ).astype(BF)
-    half = col_width // 2
-    everyone = ("row", "col", "grp")
-    count = row_count * col_count * grp_count
-    send = jnp.stack(
-        [
-            left_in.reshape(channels, 2, half, tok_rows),
-            right_in.reshape(channels, 2, half, tok_rows),
-        ],
-        axis=2,
-    ).reshape(count, 2 * half, tok_rows)
-    got = lax.all_to_all(send, everyone, 0, 0, tiled=True)
-    got = got.reshape(row_count, col_count, grp_count, 2, half, tok_rows)
+    everywhere = ("row", "col", "near")
+    count = row_count * col_count * near_count
+    send = jnp.stack([left_in, right_in], axis=1).reshape(count, 2 * col_width, tok_rows)
+    got = lax.all_to_all(send, everywhere, 0, 0, tiled=True)
+    got = got.reshape(row_count, col_count, near_count, 2, col_width, tok_rows)
     left_own, right_own = got[:, :, :, 0], got[:, :, :, 1]
-    left_other = lax.ppermute(left_own, "grp", [(i, i ^ 1) for i in range(grp_count)])
-    first = (grp_at % 2) == 0
+    left_other = lax.ppermute(left_own, "core", SWAP)
+    first = core_at == 0
     left_all = (
         jnp.stack(
             [jnp.where(first, left_own, left_other), jnp.where(first, left_other, left_own)],
             axis=3,
         )
-        .transpose(0, 2, 1, 3, 4, 5)
+        .transpose(0, 2, 3, 1, 4, 5)
         .reshape(row_count, grp_count, tok_rows, tok_rows)
     )
-    right_all = right_own.reshape(row_count, count * half // row_count, tok_rows)
+    right_all = right_own.reshape(row_count, col_count * near_count * col_width, tok_rows)
     triangle = jnp.einsum("rgik,rjk->gji", left_all, right_all, preferred_element_type=F32)
-    back = triangle.astype(BF).reshape(count, half, tok_rows)
-    tri_local = lax.all_to_all(back, everyone, 0, 0, tiled=True)
+    back = triangle.astype(BF).reshape(count, col_width, tok_rows)
+    tri_local = lax.all_to_all(back, everywhere, 0, 0, tiled=True)
     tri_local = tri_local.reshape(channels, col_width, tok_rows)
     out_normed = normalize(tri_local.astype(F32), 0).astype(BF)
     gate_out = jax.nn.sigmoid(
@@ -235,7 +244,7 @@
         bias_local.reshape(grp_count, 1, heads, col_width, tok_rows),
         (grp_count, col_count, heads, col_width, tok_rows),
     ).reshape(grp_count * col_count, heads, col_width, tok_rows)
-    bias_all = lax.all_to_all(copies, ("grp", "col"), 0, 0, tiled=True)
+    bias_all = lax.all_to_all(copies, ("near", "core", "col"), 0, 0, tiled=True)
 
     query_t = jnp.einsum("srd,de->ser", normed_x, w_qkvg[0], preferred_element_type=F32).astype(BF)
     gate_t = jax.nn.sigmoid(
@@ -252,7 +261,7 @@
             jax.ShapeDtypeStruct((samples, head_width, tok_rows), BF),
             jax.ShapeDtypeStruct((col_count, heads, keys // col_count, tok_rows), BF),
         ),
-        in_specs=[pl.BlockSpec(memory_space=pltpu.SMEM)] + [vmem] * 8,
+        in_specs=[pl.BlockSpec(memory_space=pltpu.SMEM)] + [vmem] * 9,
         out_specs=(vmem, vmem),
         scratch_shapes=[
             pltpu.VMEM((keys, head_width), BF),
@@ -271,8 +280,11 @@
         d_mixed_t,
         gate_t,
         key_value,
-        *moved,
-        bias_all,
+        from_last,
+        from_next,
+        far_top,
+        far_low,
+        pltpu.with_memory_space_constraint(bias_all, pltpu.VMEM),
     )
     gated_parts = gather_grp(gated_t, 1)
     grad_parts = lax.all_to_all(grads, "col", 0, 0, tiled=True)
@@ -289,8 +301,11 @@
 
 
 def solution(mesh):
+    grp, row, col = (mesh.shape[name] for name in ("grp", "row", "col"))
+    split = Mesh(mesh.devices.reshape(grp // 2, 2, row, col), ("near", "core", "row", "col"))
+    both = ("near", "core")
     placed = (
-        P("row", ("grp", "col"), None),
+        P("row", (*both, "col"), None),
         P(),
         P(),
         P(),
@@ -299,15 +314,15 @@
         P(),
         P(),
         P("col", "row", None),
-        P(None, None, "grp"),
-        P("grp", None),
+        P(None, None, both),
+        P(both, None),
         P("col", "row", None),
     )
 
     return jax.shard_map(
         on_device,
-        mesh=mesh,
+        mesh=split,
         in_specs=placed,
-        out_specs=(P("row", ("grp", "col"), None), P("col", "row", None), P("grp", "row", "col")),
+        out_specs=(P("row", (*both, "col"), None), P("col", "row", None), P(both, "row", "col")),
         check_vma=False,
     )

time: 160 us -> 150 us (0.938)
  blocking collectives: 34.2 us -> 0 us
  starting transfers between devices: 27.6 us -> 46 us
  waiting for transfers between devices: 60.3 us -> 68.6 us
    all_to_all x1 -> x0, blocking collectives: 34.2 us -> none  [on_device(): got = lax.all_to_all(send, everyone, 0, 0, tiled=True)]
    all_to_all x2 -> x3, waiting for transfers between devices: 14.5 us -> 34.4 us  [the longest x1 20 us: on_device(): got = lax.all_to_all(send, everywhere, 0, 0, tiled=True)]
    all_to_all x2 -> x3, starting transfers between devices: 12.5 us -> 27.8 us  [the longest x1 15.6 us: on_device(): got = lax.all_to_all(send, everywhere, 0, 0, tiled=True)]
    ppermute x8 -> x9, waiting for transfers between devices: 39.3 us -> 27.7 us  [the longest x1 18.6 us: on_device(): from_last = lax.ppermute(key_value, 'row', onward)]
    ppermute x8 -> x9, starting transfers between devices: 7.78 us -> 10.9 us  [the longest x1 3.45 us: on_device(): from_next = lax.ppermute(key_value, 'row', backward)]
    unnamed x30, local copies, waits for them, and re-layouts: 4.97 us -> 3.25 us
  transfers between devices with their start and end apart: 11 -> 13, of which waited for: 5 -> 9; matrix products, arithmetic and copies ran while one was open for 9% -> 9% of each run, Pallas kernels for 5% -> 6%
where the time goes in v1:
time: 150 us; the launch traced here: 149 us
  waiting for transfers between devices  68.6 us (46%)
  starting transfers between devices  46 us (31%)
  matrix products  13.1 us (9%)
  Pallas kernels  8.26 us (6%)
  local copies, waits for them, and re-layouts  6.74 us (4%)
  other arithmetic  5.04 us (3%)
    all_to_all x1, waiting for transfers between devices, on_device(): got = lax.all_to_all(send, everywhere, 0, 0, tiled=True)  20 us
    ppermute x1, waiting for transfers between devices, on_device(): from_last = lax.ppermute(key_value, 'row', onward)  18.6 us
    all_to_all x1, starting transfers between devices, on_device(): got = lax.all_to_all(send, everywhere, 0, 0, tiled=True)  15.6 us
    all_to_all x1, waiting for transfers between devices, on_device(): tri_local = lax.all_to_all(back, everywhere, 0, 0, tiled=True)  14.4 us
    pallas_call x1, Pallas kernels, on_device(): pl.pallas_call(lambda *refs: attention_kernel(heads, head_size, *refs), o...  8.26 us
    all_to_all x1, starting transfers between devices, on_device(): grad_parts = lax.all_to_all(grads, 'col', 0, 0, tiled=True)  7.27 us
    all_to_all x1, starting transfers between devices, on_device(): tri_local = lax.all_to_all(back, everywhere, 0, 0, tiled=True)  6.67 us
    all_to_all x1, waiting for transfers between devices, on_device(): grad_parts = lax.all_to_all(grads, 'col', 0, 0, tiled=True)  6.45 us
  transfers between devices with their start and end apart: 13, of which 9 were waited for; matrix products, arithmetic and copies ran while one was open for 9% of the time, Pallas kernels for 6%

profile of v1, /device:TPU:2, one launch (start us, length us, event | category | flops | bytes accessed | tf_op | source)
XLA Modules:
  0.0 148.6 jit_solution(9111033008278606550)
XLA Ops:
  0.7 0.8 pad_add_fusion
  1.6 1.1 copy.42
  2.8 1.0 fusion.74
  4.8 1.2 copy.46
  6.0 15.6 %all-to-all-start = ((bf16[128,16,128]{2,1,0:T(8,128)(2,1)}), bf16[128,16,128]{2,1,0:T(8,128)(2,1)S(1)}, u32[]{:S(2)}, u32[]{:S(2)}) async-start(bf16[128,16,128]{2,1,0:T(8,128)(2,1)} %copy.46), calls=%async_computation | async-start | bytes 1048576 | tf_op jit(solution)/shard_map/all_to_all | solution.py:214
  21.6 20.0 %all-to-all-done = bf16[128,16,128]{2,1,0:T(8,128)(2,1)S(1)} async-done(((bf16[128,16,128]{2,1,0:T(8,128)(2,1)}), bf16[128,16,128]{2,1,0:T(8,128)(2,1)S(1)}, u32[]{:S(2)}, u32[]{:S(2)}) %all-to-all-start) | async-done | bytes 524320 | tf_op jit(solution)/shard_map/all_to_all | solution.py:214
  42.0 1.3 collective-permute-done
  43.6 1.1 fusion.7
  44.6 6.7 %all-to-all-start.1 = ((bf16[128,8,128]{2,1,0:T(8,128)(2,1)}), bf16[128,8,128]{2,1,0:T(8,128)(2,1)S(1)}, u32[]{:S(2)}, u32[]{:S(2)}) async-start(bf16[128,8,128]{2,1,0:T(8,128)(2,1)} %bitcast.29), calls=%async_computation.1 | async-start | bytes 524288 | tf_op jit(solution)/shard_map/all_to_all | solution.py:230
  51.9 14.4 %all-to-all-done.1 = bf16[128,8,128]{2,1,0:T(8,128)(2,1)S(1)} async-done(((bf16[128,8,128]{2,1,0:T(8,128)(2,1)}), bf16[128,8,128]{2,1,0:T(8,128)(2,1)S(1)}, u32[]{:S(2)}, u32[]{:S(2)}) %all-to-all-start.1) | async-done | bytes 262176 | tf_op jit(solution)/shard_map/all_to_all | solution.py:230
  66.8 1.0 fusion.34
  68.9 1.1 broadcast_in_dim.55
  70.0 5.5 %all-to-all-start.2 = ((f32[64,4,8,128]{3,2,1,0:T(8,128)}), f32[64,4,8,128]{3,2,1,0:T(8,128)S(1)}, u32[]{:S(2)}, u32[]{:S(2)}) async-start(f32[64,4,8,128]{3,2,1,0:T(8,128)} %bitcast.50), calls=%async_computation.2 | async-start | bytes 2097152 | tf_op jit(solution)/shard_map/all_to_all | solution.py:247
  75.6 1.7 %fusion.6 = bf16[3,128,2,192]{1,3,2,0:T(8,128)(2,1)S(1)} fusion(bf16[4,768,192]{1,2,0:T(8,128)(2,1)} %param.21, bf16[3,128,768]{2,1,0:T(8,128)(2,1)S(1)} %copy-done.1, f32[3,128]{1,0:T(4,128)S(1)} %add_rsqrt_fusion.3, f32[3,128]{1,0:T(4,128)S(1)} %broadcast_multiply_fusion.3, pred[128,2]{0,1:T(4,128)(4,1)S(1)} %broadcast_or_fusion), kind=kOutput, calls=%fused_computation.14 | convolution fusion | flops 227966976 | bytes 1477888 | tf_op jit(solution)/shard_map/srd,tde->srte/dot_general | solution.py:176
  78.2 0.8 collective-permute-start.1
  79.0 3.4 %collective-permute-start.2 = (bf16[2,3,64,384]{3,2,1,0:T(8,128)(2,1)S(1)}, bf16[2,3,64,384]{3,2,1,0:T(8,128)(2,1)S(1)}, u32[]{:S(2)}, u32[]{:S(2)}) collective-permute-start(bf16[2,3,64,384]{3,2,1,0:T(8,128)(2,1)S(1)} %bitcast.147), channel_id=1, source_target_pairs={{0,48},{16,0},{32,16},{48,32},{1,49},{17,1},{33,17},{49,33},{2,50}... | collective-permute-start | bytes 884744 | tf_op jit(solution)/shard_map/ppermute | solution.py:186
  82.4 1.7 %collective-permute-start.7 = (bf16[192,768]{1,0:T(8,128)(2,1)S(1)}, bf16[192,768]{1,0:T(8,128)(2,1)S(1)}, u32[]{:S(2)}, u32[]{:S(2)}) collective-permute-start(bf16[192,768]{1,0:T(8,128)(2,1)S(1)} %copy-done.4), channel_id=1, source_target_pairs={{0,128},{128,0},{1,129},{129,1},{2,130},{130,2},{3,131},{131,3},{4... | collective-permute-start | bytes 884744 | tf_op jit(solution)/shard_map/ppermute | solution.py:26
  84.1 1.5 fusion.18.refs_3_
  85.6 1.0 fusion.19.refs_2_
  86.6 18.6 %collective-permute-done.1.refs_5_ = bf16[2,3,64,384]{3,2,1,0:T(8,128)(2,1)S(1)} collective-permute-done((bf16[2,3,64,384]{3,2,1,0:T(8,128)(2,1)S(1)}, bf16[2,3,64,384]{3,2,1,0:T(8,128)(2,1)S(1)}, u32[]{:S(2)}, u32[]{:S(2)}) %collective-permute-start.1) | collective-permute-done | bytes 294944 | tf_op jit(solution)/shard_map/ppermute | solution.py:185
  105.3 1.7 %collective-permute-start.3 = (bf16[3,64,384]{2,1,0:T(8,128)(2,1)S(1)}, bf16[3,64,384]{2,1,0:T(8,128)(2,1)S(1)}, u32[]{:S(2)}, u32[]{:S(2)}) collective-permute-start(bf16[3,64,384]{2,1,0:T(8,128)(2,1)S(1)} %slice_bitcast_fusion.2), channel_id=1, source_target_pairs={{0,16},{16,32},{32,48},{48,0},{1,17},{17,33},{33,49},{49,1},{2,18}... | collective-permute-start | bytes 442376 | tf_op jit(solution)/shard_map/ppermute | solution.py:188
  107.0 2.6 %collective-permute-start.4 = (bf16[3,64,384]{2,1,0:T(8,128)(2,1)S(1)}, bf16[3,64,384]{2,1,0:T(8,128)(2,1)S(1)}, u32[]{:S(2)}, u32[]{:S(2)}) collective-permute-start(bf16[3,64,384]{2,1,0:T(8,128)(2,1)S(1)} %slice_bitcast_fusion.1), channel_id=1, source_target_pairs={{0,48},{16,0},{32,16},{48,32},{1,49},{17,1},{33,17},{49,33},{2,50}... | collective-permute-start | bytes 442376 | tf_op jit(solution)/shard_map/ppermute | solution.py:189
  109.8 0.9 pad_maximum_fusion
  110.7 2.1 %fusion.20.refs_1_ = bf16[3,192,128]{2,1,0:T(8,128)(2,1)} fusion(bf16[3,128,768]{2,1,0:T(8,128)(2,1)S(1)} %copy-done.1, f32[3,128]{1,0:T(4,128)S(1)} %add_rsqrt_fusion.3, f32[3,128]{1,0:T(4,128)S(1)} %broadcast_multiply_fusion.3, bf16[4,768,192]{1,2,0:T(8,128)(2,1)} %param.21), kind=kOutput, calls=%fused_computation.32 | convolution fusion | flops 114499584 | bytes 1035264 | tf_op jit(solution)/shard_map/srd,de->ser/dot_general | solution.py:249
  112.8 1.4 collective-permute-done.3.refs_7_
  115.5 8.3 %attention.1 = (bf16[3,192,128]{2,1,0:T(8,128)(2,1)}, bf16[16,4,32,128]{3,2,1,0:T(8,128)(2,1)}) custom-call(s32[1]{0:T(128)} %bitcast.32.refs_0_, bf16[3,192,128]{2,1,0:T(8,128)(2,1)} %fusion.20.refs_1_, bf16[3,192,128]{2,1,0:T(8,128)(2,1)} %fusion.19.refs_2_, f32[3,192,128]{2,1,0:T(8,128)} %copy-done.3, bf16[2,3,64,384]{3,2,1,0:T(8,128)(2,1)} %bitcast.148, ...), custom_call_target="tpu_custom_call" | custom-call | tf_op jit(solution)/shard_map/attention/pallas_call | solution.py:258
  124.3 5.5 %collective-permute-done.5 = bf16[3,192,128]{2,1,0:T(8,128)(2,1)S(1)} collective-permute-done((bf16[3,192,128]{2,1,0:T(8,128)(2,1)}, bf16[3,192,128]{2,1,0:T(8,128)(2,1)S(1)}, u32[]{:S(2)}, u32[]{:S(2)}) %collective-permute-start.5) | collective-permute-done | bytes 147488 | tf_op jit(solution)/shard_map/ppermute | solution.py:26
  129.7 0.9 pad_maximum_fusion.2
  130.8 7.3 %all-to-all-start.3 = ((bf16[16,4,32,128]{3,2,1,0:T(8,128)(2,1)}), bf16[16,4,32,128]{3,2,1,0:T(8,128)(2,1)S(1)}, u32[]{:S(2)}, u32[]{:S(2)}) async-start(bf16[16,4,32,128]{3,2,1,0:T(8,128)(2,1)} %get-tuple-element.6), calls=%async_computation.3 | async-start | bytes 1048576 | tf_op jit(solution)/shard_map/all_to_all | solution.py:290
  138.0 0.9 copy.55
  138.9 2.5 %fusion.2 = bf16[3,128,768]{2,1,0:T(8,128)(2,1)} fusion(bf16[3,128,768]{2,1,0:T(8,128)(2,1)S(1)} %copy-done.1, bf16[384,768]{1,0:T(8,128)(2,1)} %collective-permute-done.8, bf16[192,768]{1,0:T(8,128)(2,1)S(1)} %collective-permute-done.7, bf16[192,768]{1,0:T(8,128)(2,1)S(1)} %copy-done.4, bf16[3,384,128]{2,1,0:T(8,128)(2,1)S(1)} %collective-permute-done.6, ...), kind=kOutput, calls=%fused_computation.6 | convolution fusion | flops 459177984 | bytes 2949120 | tf_op jit(solution)/shard_map/ser,ed->srd/dot_general | solution.py:293
  141.5 6.4 %all-to-all-done.3 = bf16[16,4,32,128]{3,2,1,0:T(8,128)(2,1)S(1)} async-done(((bf16[16,4,32,128]{3,2,1,0:T(8,128)(2,1)}), bf16[16,4,32,128]{3,2,1,0:T(8,128)(2,1)S(1)}, u32[]{:S(2)}, u32[]{:S(2)}) %all-to-all-start.3) | async-done | bytes 524320 | tf_op jit(solution)/shard_map/all_to_all | solution.py:290
  (78 shorter events, 7.7 us)
Async XLA Ops:
  0.6 84.9 %copy-start = (bf16[3,128,768]{2,1,0:T(8,128)(2,1)S(1)}, bf16[3,128,768]{2,1,0:T(8,128)(2,1)}, u32[]{:S(2)}) copy-start(bf16[3,128,768]{2,1,0:T(8,128)(2,1)} %param.23) | copy-start | bytes 1769476
  0.6 3.3 %copy-start.11 = (bf16[128,640]{1,0:T(8,128)(2,1)S(1)}, bf16[128,640]{1,0:T(8,128)(2,1)}, u32[]{:S(2)}) copy-start(bf16[128,640]{1,0:T(8,128)(2,1)} %param.17) | copy-start | bytes 491524
  6.0 35.8 %copy-start.1 = (bf16[3,128,768]{2,1,0:T(8,128)(2,1)S(1)}, bf16[3,128,768]{2,1,0:T(8,128)(2,1)}, u32[]{:S(2)}) copy-start(bf16[3,128,768]{2,1,0:T(8,128)(2,1)} %param.20) | copy-start | bytes 1769476
  6.0 35.6 %all-to-all-start = ((bf16[128,16,128]{2,1,0:T(8,128)(2,1)}), bf16[128,16,128]{2,1,0:T(8,128)(2,1)S(1)}, u32[]{:S(2)}, u32[]{:S(2)}) async-start(bf16[128,16,128]{2,1,0:T(8,128)(2,1)} %copy.46), calls=%async_computation | async-start | bytes 1048576 | tf_op jit(solution)/shard_map/all_to_all | solution.py:214
  41.7 1.6 %collective-permute-start = (bf16[4,16,2,8,128]{4,3,2,1,0:T(8,128)(2,1)S(1)}, bf16[4,16,2,8,128]{4,3,2,1,0:T(8,128)(2,1)S(1)}, u32[]{:S(2)}, u32[]{:S(2)}) collective-permute-start(bf16[4,16,2,8,128]{4,3,2,1,0:T(8,128)(2,1)S(1)} %get-tuple-element.22), channel_id=1, source_target_pairs={{0,64},{64,0},{1,65},{65,1},{2,66},{66,2},{3,67},{67,3},{4,68},{68... | collective-permute-start | bytes 786440 | tf_op jit(solution)/shard_map/ppermute | solution.py:217
  44.6 21.8 %all-to-all-start.1 = ((bf16[128,8,128]{2,1,0:T(8,128)(2,1)}), bf16[128,8,128]{2,1,0:T(8,128)(2,1)S(1)}, u32[]{:S(2)}, u32[]{:S(2)}) async-start(bf16[128,8,128]{2,1,0:T(8,128)(2,1)} %bitcast.29), calls=%async_computation.1 | async-start | bytes 524288 | tf_op jit(solution)/shard_map/all_to_all | solution.py:230
  51.6 15.1 %copy-start.12 = (bf16[128,128]{1,0:T(8,128)(2,1)S(1)}, bf16[128,128]{1,0:T(8,128)(2,1)}, u32[]{:S(2)}) copy-start(bf16[128,128]{1,0:T(8,128)(2,1)} %param.18) | copy-start | bytes 98308
  67.7 0.7 copy-start.13
  70.0 44.8 %all-to-all-start.2 = ((f32[64,4,8,128]{3,2,1,0:T(8,128)}), f32[64,4,8,128]{3,2,1,0:T(8,128)S(1)}, u32[]{:S(2)}, u32[]{:S(2)}) async-start(f32[64,4,8,128]{3,2,1,0:T(8,128)} %bitcast.50), calls=%async_computation.2 | async-start | bytes 2097152 | tf_op jit(solution)/shard_map/all_to_all | solution.py:247
  77.3 5.1 %copy-start.4 = (bf16[192,768]{1,0:T(8,128)(2,1)S(1)}, bf16[192,768]{1,0:T(8,128)(2,1)}, u32[]{:S(2)}) copy-start(bf16[192,768]{1,0:T(8,128)(2,1)} %param.22) | copy-start | bytes 884740
  78.2 7.4 %copy-start.2 = (bf16[3,2,64,384]{3,2,0,1:T(8,128)(2,1)}, bf16[3,2,64,384]{3,2,0,1:T(8,128)(2,1)S(1)}, u32[]{:S(2)}) copy-start(bf16[3,2,64,384]{3,2,0,1:T(8,128)(2,1)S(1)} %copy.51) | copy-start | bytes 884740
  78.2 27.0 %collective-permute-start.1 = (bf16[2,3,64,384]{3,2,1,0:T(8,128)(2,1)S(1)}, bf16[2,3,64,384]{3,2,1,0:T(8,128)(2,1)S(1)}, u32[]{:S(2)}, u32[]{:S(2)}) collective-permute-start(bf16[2,3,64,384]{3,2,1,0:T(8,128)(2,1)S(1)} %bitcast.146), channel_id=1, source_target_pairs={{0,16},{16,32},{32,48},{48,0},{1,17},{17,33},{33,49},{49,1},{2,18}... | collective-permute-start | bytes 884744 | tf_op jit(solution)/shard_map/ppermute | solution.py:185
  79.0 28.0 %collective-permute-start.2 = (bf16[2,3,64,384]{3,2,1,0:T(8,128)(2,1)S(1)}, bf16[2,3,64,384]{3,2,1,0:T(8,128)(2,1)S(1)}, u32[]{:S(2)}, u32[]{:S(2)}) collective-permute-start(bf16[2,3,64,384]{3,2,1,0:T(8,128)(2,1)S(1)} %bitcast.147), channel_id=1, source_target_pairs={{0,48},{16,0},{32,16},{48,32},{1,49},{17,1},{33,17},{49,33},{2,50}... | collective-permute-start | bytes 884744 | tf_op jit(solution)/shard_map/ppermute | solution.py:186
  82.4 27.4 %collective-permute-start.7 = (bf16[192,768]{1,0:T(8,128)(2,1)S(1)}, bf16[192,768]{1,0:T(8,128)(2,1)S(1)}, u32[]{:S(2)}, u32[]{:S(2)}) collective-permute-start(bf16[192,768]{1,0:T(8,128)(2,1)S(1)} %copy-done.4), channel_id=1, source_target_pairs={{0,128},{128,0},{1,129},{129,1},{2,130},{130,2},{3,131},{131,3},{4... | collective-permute-start | bytes 884744 | tf_op jit(solution)/shard_map/ppermute | solution.py:26
  85.6 25.1 %copy-start.3 = (f32[3,192,128]{2,1,0:T(8,128)}, f32[3,192,128]{2,1,0:T(8,128)S(1)}, u32[]{:S(2)}) copy-start(f32[3,192,128]{2,1,0:T(8,128)S(1)} %fusion.18.refs_3_) | copy-start | bytes 884740
  105.2 7.5 %copy-start.6 = (bf16[2,3,64,384]{3,2,1,0:T(8,128)(2,1)}, bf16[2,3,64,384]{3,2,1,0:T(8,128)(2,1)S(1)}, u32[]{:S(2)}) copy-start(bf16[2,3,64,384]{3,2,1,0:T(8,128)(2,1)S(1)} %collective-permute-done.1.refs_5_) | copy-start | bytes 884740
  105.3 8.9 %collective-permute-start.3 = (bf16[3,64,384]{2,1,0:T(8,128)(2,1)S(1)}, bf16[3,64,384]{2,1,0:T(8,128)(2,1)S(1)}, u32[]{:S(2)}, u32[]{:S(2)}) collective-permute-start(bf16[3,64,384]{2,1,0:T(8,128)(2,1)S(1)} %slice_bitcast_fusion.2), channel_id=1, source_target_pairs={{0,16},{16,32},{32,48},{48,0},{1,17},{17,33},{33,49},{49,1},{2,18}... | collective-permute-start | bytes 442376 | tf_op jit(solution)/shard_map/ppermute | solution.py:188
  107.0 5.8 %copy-start.7 = (bf16[2,3,64,384]{3,2,1,0:T(8,128)(2,1)}, bf16[2,3,64,384]{3,2,1,0:T(8,128)(2,1)S(1)}, u32[]{:S(2)}) copy-start(bf16[2,3,64,384]{3,2,1,0:T(8,128)(2,1)S(1)} %collective-permute-done.2.refs_6_) | copy-start | bytes 884740
  107.0 7.8 %collective-permute-start.4 = (bf16[3,64,384]{2,1,0:T(8,128)(2,1)S(1)}, bf16[3,64,384]{2,1,0:T(8,128)(2,1)S(1)}, u32[]{:S(2)}, u32[]{:S(2)}) collective-permute-start(bf16[3,64,384]{2,1,0:T(8,128)(2,1)S(1)} %slice_bitcast_fusion.1), channel_id=1, source_target_pairs={{0,48},{16,0},{32,16},{48,32},{1,49},{17,1},{33,17},{49,33},{2,50}... | collective-permute-start | bytes 442376 | tf_op jit(solution)/shard_map/ppermute | solution.py:189
  110.7 28.2 %collective-permute-start.8 = (bf16[384,768]{1,0:T(8,128)(2,1)}, bf16[384,768]{1,0:T(8,128)(2,1)}, u32[]{:S(2)}, u32[]{:S(2)}) collective-permute-start(bf16[384,768]{1,0:T(8,128)(2,1)} %pad_maximum_fusion), channel_id=1, source_target_pairs={{0,64},{64,0},{1,65},{65,1},{2,66},{66,2},{3,67},{67,3},{4,68},{68... | collective-permute-start | bytes 1769480 | tf_op jit(solution)/shard_map/ppermute | solution.py:28
  114.2 0.7 copy-start.8
  114.8 0.7 copy-start.9
  123.7 14.3 %copy-start.5 = (bf16[128,8,128]{0,2,1:T(8,128)(2,1)S(1)}, bf16[128,8,128]{0,2,1:T(8,128)(2,1)}, u32[]{:S(2)}) copy-start(bf16[128,8,128]{0,2,1:T(8,128)(2,1)} %get-tuple-element.32) | copy-start | bytes 786436
  123.7 15.2 %copy-start.10 = (bf16[3,192,128]{2,1,0:T(8,128)(2,1)S(1)}, bf16[3,192,128]{2,1,0:T(8,128)(2,1)}, u32[]{:S(2)}) copy-start(bf16[3,192,128]{2,1,0:T(8,128)(2,1)} %get-tuple-element.5) | copy-start | bytes 442372
  123.7 6.0 %collective-permute-start.5 = (bf16[3,192,128]{2,1,0:T(8,128)(2,1)}, bf16[3,192,128]{2,1,0:T(8,128)(2,1)S(1)}, u32[]{:S(2)}, u32[]{:S(2)}) collective-permute-start(bf16[3,192,128]{2,1,0:T(8,128)(2,1)} %get-tuple-element.5), channel_id=1, source_target_pairs={{0,128},{128,0},{1,129},{129,1},{2,130},{130,2},{3,131},{131,3},{4... | collective-permute-start | bytes 442376 | tf_op jit(solution)/shard_map/ppermute | solution.py:26
  130.7 8.3 %collective-permute-start.6 = (bf16[3,384,128]{2,1,0:T(8,128)(2,1)S(1)}, bf16[3,384,128]{2,1,0:T(8,128)(2,1)S(1)}, u32[]{:S(2)}, u32[]{:S(2)}) collective-permute-start(bf16[3,384,128]{2,1,0:T(8,128)(2,1)S(1)} %pad_maximum_fusion.2), channel_id=1, source_target_pairs={{0,64},{64,0},{1,65},{65,1},{2,66},{66,2},{3,67},{67,3},{4,68},{68... | collective-permute-start | bytes 884744 | tf_op jit(solution)/shard_map/ppermute | solution.py:28
  130.8 17.2 %all-to-all-start.3 = ((bf16[16,4,32,128]{3,2,1,0:T(8,128)(2,1)}), bf16[16,4,32,128]{3,2,1,0:T(8,128)(2,1)S(1)}, u32[]{:S(2)}, u32[]{:S(2)}) async-start(bf16[16,4,32,128]{3,2,1,0:T(8,128)(2,1)} %get-tuple-element.6), calls=%async_computation.3 | async-start | bytes 1048576 | tf_op jit(solution)/shard_map/all_to_all | solution.py:290

commit v2 on v1

--- a/solution.py
+++ b/solution.py
@@ -10,6 +10,8 @@
 
 BF = jnp.bfloat16
 F32 = jnp.float32
+LOG2E = 1.4426950408889634
+HIDDEN = -65504.0
 
 
 def normalize(values, axis_at):
@@ -55,13 +57,15 @@
 ):
     samples, width, rows = qt_ref.shape
     row_count = 4
-    keys = rows * row_count
-    scale = 1.0 / math.sqrt(head_size)
+    scale = LOG2E / math.sqrt(head_size)
     row_at = row_ref[0]
     qbd[...] = jnp.zeros_like(qbd)
     dbd[...] = jnp.zeros_like(dbd)
-    chunk = 64
-    groups = chunk // 8
+    gacc[...] = jnp.zeros_like(gacc)
+    tiles = rows // 8
+
+    def fold(x, op):
+        return op(x.reshape(tiles, 8, 2 * rows), axis=0)
 
     def one_sample(s, unused):
         for step, halves in enumerate(
@@ -81,51 +85,44 @@
             e0, i0 = h * head_size, h * rows
             qbd[e0 : e0 + head_size, i0 : i0 + rows] = qt_ref[s, e0 : e0 + head_size, :]
             dbd[e0 : e0 + head_size, i0 : i0 + rows] = dmt_ref[s, e0 : e0 + head_size, :]
-        st[...] = jnp.dot(k_s[...], qbd[...], preferred_element_type=F32)
-        dpt[...] = jnp.dot(v_s[...], dbd[...], preferred_element_type=F32)
+        for h in range(0, heads, 2):
+            lanes = slice(h * rows, (h + 2) * rows)
+            top = jnp.full((8, 2 * rows), -jnp.inf, F32)
+            for b in range(row_count):
+                part = slice(b * rows, (b + 1) * rows)
+                places = slice(b * tiles, (b + 1) * tiles)
+                bias = jnp.concatenate(
+                    [bias_ref[places, h + n, :, :].reshape(rows, rows) for n in range(2)], axis=1
+                )
+                x = jnp.dot(k_s[part, :], qbd[:, lanes], preferred_element_type=F32)
+                x = x * scale + bias
+                st[part, lanes] = x
+                top = jnp.maximum(top, fold(x, jnp.max))
+            peak = jnp.max(top, axis=0, keepdims=True)
+            total = jnp.zeros((8, 2 * rows), F32)
+            dots = jnp.zeros((8, 2 * rows), F32)
+            for b in range(row_count):
+                part = slice(b * rows, (b + 1) * rows)
+                d = jnp.dot(v_s[part, :], dbd[:, lanes], preferred_element_type=F32)
+                w = jnp.exp2(st[part, lanes] - peak)
+                st[part, lanes] = w
+                dpt[part, lanes] = d
+                total = total + fold(w, jnp.sum)
+                dots = dots + fold(w * d, jnp.sum)
+            inverse = 1.0 / jnp.sum(total, axis=0, keepdims=True)
+            inner = jnp.sum(dots, axis=0, keepdims=True) * inverse
+            for b in range(row_count):
+                part = slice(b * rows, (b + 1) * rows)
+                p = st[part, lanes] * inverse
+                pt[part, lanes] = p.astype(BF)
+                gacc[part, lanes] = gacc[part, lanes] + p * (dpt[part, lanes] - inner)
+        mixed = lax.dot_general(
+            v_s[...], pt[...], (((0,), (0,)), ((), ())), preferred_element_type=F32
+        )
         for h in range(heads):
             e0, i0 = h * head_size, h * rows
-            lanes = slice(i0, i0 + rows)
-            top = jnp.full((8, rows), -jnp.inf, F32)
-            for b in range(keys // chunk):
-                part = slice(b * chunk, (b + 1) * chunk)
-                bias = bias_ref[b * groups : (b + 1) * groups, h, :, :].reshape(chunk, rows)
-                x = st[part, lanes] * scale + bias
-                st[part, lanes] = x
-                top = jnp.maximum(top, jnp.max(x.reshape(groups, 8, rows), axis=0))
-            peak = jnp.max(top, axis=0, keepdims=True)
-            total = jnp.zeros((8, rows), F32)
-            dots = jnp.zeros((8, rows), F32)
-            for b in range(keys // chunk):
-                part = slice(b * chunk, (b + 1) * chunk)
-                w = jnp.exp(st[part, lanes] - peak)
-                st[part, lanes] = w
-                total = total + jnp.sum(w.reshape(groups, 8, rows), axis=0)
-                dots = dots + jnp.sum((w * dpt[part, lanes]).reshape(groups, 8, rows), axis=0)
-            inverse = 1.0 / jnp.sum(total, axis=0, keepdims=True)
-            inner = jnp.sum(dots, axis=0, keepdims=True) * inverse
-            for b in range(keys // chunk):
-                part = slice(b * chunk, (b + 1) * chunk)
-                p = st[part, lanes] * inverse
-                pt[part, lanes] = p.astype(BF)
-                d = p * (dpt[part, lanes] - inner)
-
-                @pl.when(s == 0)
-                def _():
-                    gacc[h, part, :] = d
-
-                @pl.when(s > 0)
-                def _():
-                    gacc[h, part, :] = gacc[h, part, :] + d
-
-            mixed = lax.dot_general(
-                v_s[...],
-                pt[:, lanes],
-                (((0,), (0,)), ((), ())),
-                preferred_element_type=F32,
-            )
             gated_ref[s, e0 : e0 + head_size, :] = (
-                mixed[e0 : e0 + head_size, :] * gt_ref[s, e0 : e0 + head_size, :]
+                mixed[e0 : e0 + head_size, i0 : i0 + rows] * gt_ref[s, e0 : e0 + head_size, :]
             ).astype(BF)
         return unused
 
@@ -133,7 +130,9 @@
     parts, _, width_j, _ = grad_ref.shape
     for h in range(heads):
         for c in range(parts):
-            grad_ref[c, h, :, :] = gacc[h, c * width_j : (c + 1) * width_j, :].astype(BF)
+            grad_ref[c, h, :, :] = gacc[
+                c * width_j : (c + 1) * width_j, h * rows : (h + 1) * rows
+            ].astype(BF)
 
 
 def on_device(
@@ -230,6 +229,7 @@
     tri_local = lax.all_to_all(back, everywhere, 0, 0, tiled=True)
     tri_local = tri_local.reshape(channels, col_width, tok_rows)
     out_normed = normalize(tri_local.astype(F32), 0).astype(BF)
+    bias_scaled = lax.optimization_barrier(bias_weight * LOG2E)
     gate_out = jax.nn.sigmoid(
         jnp.einsum("jic,cd->jid", normed, proj_in[:, 4 * channels :], preferred_element_type=F32)
     )
@@ -237,14 +237,16 @@
     pair_new = pair_in + gate_out * update
     pair_out = pair_new.astype(BF).transpose(1, 0, 2)
     bias_local = jnp.einsum(
-        "jic,ch->hji", normalize(pair_new, 2), bias_weight, precision=lax.Precision.HIGHEST
-    )
-    bias_local = jnp.where((mask_cols == 1)[None, :, None], bias_local, -1000000000.0)
+        "jic,ch->hji", normalize(pair_new, 2), bias_scaled, precision=lax.Precision.HIGHEST
+    )
+    bias_local = jnp.where((mask_cols == 1)[None, :, None], bias_local, HIDDEN).astype(jnp.float16)
     copies = jnp.broadcast_to(
         bias_local.reshape(grp_count, 1, heads, col_width, tok_rows),
         (grp_count, col_count, heads, col_width, tok_rows),
     ).reshape(grp_count * col_count, heads, col_width, tok_rows)
     bias_all = lax.all_to_all(copies, ("near", "core", "col"), 0, 0, tiled=True)
+    bias_all = bias_all.astype(F32)
+    bias_all = jnp.where(bias_all > 0.5 * HIDDEN, bias_all, -1000000000.0 * LOG2E)
 
     query_t = jnp.einsum("srd,de->ser", normed_x, w_qkvg[0], preferred_element_type=F32).astype(BF)
     gate_t = jax.nn.sigmoid(
@@ -271,7 +273,7 @@
             pltpu.VMEM((keys, heads * tok_rows), F32),
             pltpu.VMEM((keys, heads * tok_rows), F32),
             pltpu.VMEM((keys, heads * tok_rows), BF),
-            pltpu.VMEM((heads, keys, tok_rows), F32),
+            pltpu.VMEM((keys, heads * tok_rows), F32),
         ],
         name="attention",
     )(

time: 150 us -> 139 us (0.927)
  the two profiles are of different devices: /device:TPU:2 before, /device:TPU:64 now
where the time goes in v2:
time: 139 us; the launch traced here: 138 us
  waiting for transfers between devices  54 us (39%)
  starting transfers between devices  46 us (33%)
  matrix products  13.2 us (9%)
  local copies, waits for them, and re-layouts  10.7 us (8%)
  other arithmetic  7.8 us (6%)
  Pallas kernels  5.25 us (4%)
    all_to_all x1, waiting for transfers between devices, on_device(): got = lax.all_to_all(send, everywhere, 0, 0, tiled=True)  18.4 us
    all_to_all x1, starting transfers between devices, on_device(): got = lax.all_to_all(send, everywhere, 0, 0, tiled=True)  14.7 us
    all_to_all x1, waiting for transfers between devices, on_device(): tri_local = lax.all_to_all(back, everywhere, 0, 0, tiled=True)  12.7 us
    all_to_all x1, starting transfers between devices, on_device(): tri_local = lax.all_to_all(back, everywhere, 0, 0, tiled=True)  9.29 us
    all_to_all x1, waiting for transfers between devices, on_device(): grad_parts = lax.all_to_all(grads, 'col', 0, 0, tiled=True)  8.63 us
    all_to_all x1, starting transfers between devices, on_device(): grad_parts = lax.all_to_all(grads, 'col', 0, 0, tiled=True)  6.98 us
    all_to_all x1, starting transfers between devices, on_device(): bias_all = lax.all_to_all(copies, ('near', 'core', 'col'), 0, 0, tiled=True)  6.82 us
    ppermute x1, waiting for transfers between devices, on_device(): far_low = lax.ppermute(next_half, 'row', backward)  5.96 us
  transfers between devices with their start and end apart: 13, of which 6 were waited for; matrix products, arithmetic and copies ran while one was open for 17% of the time, Pallas kernels for 4%

profile of v2, /device:TPU:64, one launch (start us, length us, event | category | flops | bytes accessed | tf_op | source)
XLA Modules:
  0.0 137.9 jit_solution(10791160203484470322)
XLA Ops:
  0.7 0.8 pad_add_fusion
  1.6 1.1 copy.42
  2.8 1.0 fusion.75
  4.8 1.2 copy.46
  6.0 14.7 %all-to-all-start = ((bf16[128,16,128]{2,1,0:T(8,128)(2,1)}), bf16[128,16,128]{2,1,0:T(8,128)(2,1)S(1)}, u32[]{:S(2)}, u32[]{:S(2)}) async-start(bf16[128,16,128]{2,1,0:T(8,128)(2,1)} %copy.46), calls=%async_computation | async-start | bytes 1048576 | tf_op jit(solution)/shard_map/all_to_all | solution.py:213
  21.3 18.4 %all-to-all-done = bf16[128,16,128]{2,1,0:T(8,128)(2,1)S(1)} async-done(((bf16[128,16,128]{2,1,0:T(8,128)(2,1)}), bf16[128,16,128]{2,1,0:T(8,128)(2,1)S(1)}, u32[]{:S(2)}, u32[]{:S(2)}) %all-to-all-start) | async-done | bytes 524320 | tf_op jit(solution)/shard_map/all_to_all | solution.py:213
  39.6 0.9 slice_bitcast_fusion
  40.5 1.7 %fusion.6 = bf16[3,128,2,192]{1,3,2,0:T(8,128)(2,1)S(1)} fusion(bf16[4,768,192]{1,2,0:T(8,128)(2,1)} %param.21, bf16[3,128,768]{2,1,0:T(8,128)(2,1)S(1)} %copy-done.1, f32[3,128]{1,0:T(4,128)S(1)} %add_rsqrt_fusion.3, f32[3,128]{1,0:T(4,128)S(1)} %broadcast_multiply_fusion.4, pred[128,2]{0,1:T(4,128)(4,1)S(1)} %broadcast_or_fusion), kind=kOutput, calls=%fused_computation.15 | convolution fusion | flops 227966976 | bytes 1477888 | tf_op jit(solution)/shard_map/srd,tde->srte/dot_general | solution.py:175
  43.8 2.2 %collective-permute-start.2 = (bf16[2,3,64,384]{3,2,1,0:T(8,128)(2,1)S(1)}, bf16[2,3,64,384]{3,2,1,0:T(8,128)(2,1)}, u32[]{:S(2)}, u32[]{:S(2)}) collective-permute-start(bf16[2,3,64,384]{3,2,1,0:T(8,128)(2,1)S(1)} %bitcast.145), channel_id=1, source_target_pairs={{0,48},{16,0},{32,16},{48,32},{1,49},{17,1},{33,17},{49,33},{2,50}... | collective-permute-start | bytes 884744 | tf_op jit(solution)/shard_map/ppermute | solution.py:185
  47.2 1.0 select_bitcast_fusion.1
  49.1 1.0 fusion.7
  50.2 9.3 %all-to-all-start.1 = ((bf16[128,8,128]{2,1,0:T(8,128)(2,1)}), bf16[128,8,128]{2,1,0:T(8,128)(2,1)S(1)}, u32[]{:S(2)}, u32[]{:S(2)}) async-start(bf16[128,8,128]{2,1,0:T(8,128)(2,1)} %bitcast.29), calls=%async_computation.1 | async-start | bytes 524288 | tf_op jit(solution)/shard_map/all_to_all | solution.py:229
  59.5 1.5 %fusion.18.refs_3_ = f32[3,192,128]{2,1,0:T(8,128)S(1)} fusion(bf16[3,128,768]{2,1,0:T(8,128)(2,1)S(1)} %copy-done.1, f32[3,128]{1,0:T(4,128)S(1)} %copy-done.12, f32[3,128]{1,0:T(4,128)S(1)} %broadcast_multiply_fusion.4, bf16[4,768,192]{1,2,0:T(8,128)(2,1)} %param.21), kind=kOutput, calls=%fused_computation.30 | convolution fusion | flops 114647040 | bytes 1182720 | tf_op jit(solution)/shard_map/srd,de->ser/dot_general | solution.py:253
  61.0 1.1 fusion.5
  62.1 12.7 %all-to-all-done.1 = bf16[128,8,128]{2,1,0:T(8,128)(2,1)S(1)} async-done(((bf16[128,8,128]{2,1,0:T(8,128)(2,1)}), bf16[128,8,128]{2,1,0:T(8,128)(2,1)S(1)}, u32[]{:S(2)}, u32[]{:S(2)}) %all-to-all-start.1) | async-done | bytes 262176 | tf_op jit(solution)/shard_map/all_to_all | solution.py:229
  76.8 0.9 broadcast_in_dim.59
  77.6 6.8 %all-to-all-start.2 = ((f16[64,4,8,128]{3,2,1,0:T(8,128)(2,1)}), f16[64,4,8,128]{3,2,1,0:T(8,128)(2,1)S(1)}, u32[]{:S(2)}, u32[]{:S(2)}) async-start(f16[64,4,8,128]{3,2,1,0:T(8,128)(2,1)} %bitcast.49), calls=%async_computation.2 | async-start | bytes 1048576 | tf_op jit(solution)/shard_map/all_to_all | solution.py:247
  84.5 1.0 fusion.19.refs_2_
  85.5 2.1 %fusion.20.refs_1_ = bf16[3,192,128]{2,1,0:T(8,128)(2,1)} fusion(bf16[3,128,768]{2,1,0:T(8,128)(2,1)S(1)} %copy-done.1, f32[3,128]{1,0:T(4,128)S(1)} %copy-done.12, f32[3,128]{1,0:T(4,128)S(1)} %broadcast_multiply_fusion.4, bf16[4,768,192]{1,2,0:T(8,128)(2,1)} %param.21), kind=kOutput, calls=%fused_computation.33 | convolution fusion | flops 114499584 | bytes 1035264 | tf_op jit(solution)/shard_map/srd,de->ser/dot_general | solution.py:251
  87.6 1.6 %slice_bitcast_fusion.2 = bf16[3,64,384]{2,1,0:T(8,128)(2,1)} fusion(bf16[2,3,64,384]{3,2,1,0:T(8,128)(2,1)} %collective-permute-done.1.refs_5_), kind=kLoop, calls=%fused_computation.95 | loop fusion | bytes 294912 | tf_op jit(solution)/shard_map/squeeze | solution.py:186
  89.2 4.5 %collective-permute-start.3 = (bf16[3,64,384]{2,1,0:T(8,128)(2,1)}, bf16[3,64,384]{2,1,0:T(8,128)(2,1)S(1)}, u32[]{:S(2)}, u32[]{:S(2)}) collective-permute-start(bf16[3,64,384]{2,1,0:T(8,128)(2,1)} %slice_bitcast_fusion.2), channel_id=1, source_target_pairs={{0,16},{16,32},{32,48},{48,0},{1,17},{17,33},{33,49},{49,1},{2,18}... | collective-permute-start | bytes 442376 | tf_op jit(solution)/shard_map/ppermute | solution.py:187
  93.7 1.6 %slice_bitcast_fusion.1 = bf16[3,64,384]{2,1,0:T(8,128)(2,1)} fusion(bf16[2,3,64,384]{3,2,1,0:T(8,128)(2,1)} %collective-permute-done.2.refs_6_), kind=kLoop, calls=%fused_computation.94 | loop fusion | bytes 294912 | tf_op jit(solution)/shard_map/squeeze | solution.py:186
  95.3 1.8 %pad_maximum_fusion = bf16[384,768]{1,0:T(8,128)(2,1)} fusion(bf16[192,768]{1,0:T(8,128)(2,1)} %collective-permute-done.7, bf16[192,768]{1,0:T(8,128)(2,1)S(1)} %copy-done.4), kind=kLoop, calls=%fused_computation.48 | loop fusion | flops 1179648 | bytes 1179648 | tf_op jit(solution)/shard_map/concatenate | solution.py:29
  97.3 3.2 %collective-permute-done.3.refs_7_ = bf16[3,64,384]{2,1,0:T(8,128)(2,1)S(1)} collective-permute-done((bf16[3,64,384]{2,1,0:T(8,128)(2,1)}, bf16[3,64,384]{2,1,0:T(8,128)(2,1)S(1)}, u32[]{:S(2)}, u32[]{:S(2)}) %collective-permute-start.3) | collective-permute-done | bytes 147488 | tf_op jit(solution)/shard_map/ppermute | solution.py:187
  100.5 6.0 %collective-permute-done.4.refs_8_ = bf16[3,64,384]{2,1,0:T(8,128)(2,1)} collective-permute-done((bf16[3,64,384]{2,1,0:T(8,128)(2,1)}, bf16[3,64,384]{2,1,0:T(8,128)(2,1)}, u32[]{:S(2)}, u32[]{:S(2)}) %collective-permute-start.4) | collective-permute-done | bytes 147488 | tf_op jit(solution)/shard_map/ppermute | solution.py:188
  106.4 5.2 %attention.1 = (bf16[3,192,128]{2,1,0:T(8,128)(2,1)}, bf16[16,4,32,128]{3,2,1,0:T(8,128)(2,1)}) custom-call(s32[1]{0:T(128)} %bitcast.32.refs_0_, bf16[3,192,128]{2,1,0:T(8,128)(2,1)} %fusion.20.refs_1_, bf16[3,192,128]{2,1,0:T(8,128)(2,1)} %fusion.19.refs_2_, f32[3,192,128]{2,1,0:T(8,128)} %copy-done.3, bf16[2,3,64,384]{3,2,1,0:T(8,128)(2,1)} %bitcast.146, ...), custom_call_target="tpu_custom_call" | custom-call | tf_op jit(solution)/shard_map/attention/pallas_call | solution.py:260
  111.9 5.1 %collective-permute-done.5 = bf16[3,192,128]{2,1,0:T(8,128)(2,1)S(1)} collective-permute-done((bf16[3,192,128]{2,1,0:T(8,128)(2,1)}, bf16[3,192,128]{2,1,0:T(8,128)(2,1)S(1)}, u32[]{:S(2)}, u32[]{:S(2)}) %collective-permute-start.5) | collective-permute-done | bytes 147488 | tf_op jit(solution)/shard_map/ppermute | solution.py:28
  117.0 0.9 pad_maximum_fusion.2
  118.1 7.0 %all-to-all-start.3 = ((bf16[16,4,32,128]{3,2,1,0:T(8,128)(2,1)}), bf16[16,4,32,128]{3,2,1,0:T(8,128)(2,1)S(1)}, u32[]{:S(2)}, u32[]{:S(2)}) async-start(bf16[16,4,32,128]{3,2,1,0:T(8,128)(2,1)} %get-tuple-element.6), calls=%async_computation.3 | async-start | bytes 1048576 | tf_op jit(solution)/shard_map/all_to_all | solution.py:292
  125.1 0.9 copy.55
  125.9 2.6 %fusion.2 = bf16[3,128,768]{2,1,0:T(8,128)(2,1)} fusion(bf16[3,128,768]{2,1,0:T(8,128)(2,1)S(1)} %copy-done.1, bf16[384,768]{1,0:T(8,128)(2,1)} %collective-permute-done.8, bf16[192,768]{1,0:T(8,128)(2,1)} %collective-permute-done.7, bf16[192,768]{1,0:T(8,128)(2,1)S(1)} %copy-done.4, bf16[3,384,128]{2,1,0:T(8,128)(2,1)S(1)} %collective-permute-done.6, ...), kind=kOutput, calls=%fused_computation.7 | convolution fusion | flops 459177984 | bytes 2949120 | tf_op jit(solution)/shard_map/ser,ed->srd/dot_general | solution.py:295
  128.6 8.6 %all-to-all-done.3 = bf16[16,4,32,128]{3,2,1,0:T(8,128)(2,1)S(1)} async-done(((bf16[16,4,32,128]{3,2,1,0:T(8,128)(2,1)}), bf16[16,4,32,128]{3,2,1,0:T(8,128)(2,1)S(1)}, u32[]{:S(2)}, u32[]{:S(2)}) %all-to-all-start.3) | async-done | bytes 524320 | tf_op jit(solution)/shard_map/all_to_all | solution.py:292
  (78 shorter events, 8.4 us)
Async XLA Ops:
  0.6 83.9 %copy-start = (bf16[3,128,768]{2,1,0:T(8,128)(2,1)S(1)}, bf16[3,128,768]{2,1,0:T(8,128)(2,1)}, u32[]{:S(2)}) copy-start(bf16[3,128,768]{2,1,0:T(8,128)(2,1)} %param.23) | copy-start | bytes 1769476
  0.6 3.3 %copy-start.9 = (bf16[128,640]{1,0:T(8,128)(2,1)S(1)}, bf16[128,640]{1,0:T(8,128)(2,1)}, u32[]{:S(2)}) copy-start(bf16[128,640]{1,0:T(8,128)(2,1)} %param.17) | copy-start | bytes 491524
  4.8 15.9 %copy-start.1 = (bf16[3,128,768]{2,1,0:T(8,128)(2,1)S(1)}, bf16[3,128,768]{2,1,0:T(8,128)(2,1)}, u32[]{:S(2)}) copy-start(bf16[3,128,768]{2,1,0:T(8,128)(2,1)} %param.20) | copy-start | bytes 1769476
  6.0 33.6 %all-to-all-start = ((bf16[128,16,128]{2,1,0:T(8,128)(2,1)}), bf16[128,16,128]{2,1,0:T(8,128)(2,1)S(1)}, u32[]{:S(2)}, u32[]{:S(2)}) async-start(bf16[128,16,128]{2,1,0:T(8,128)(2,1)} %copy.46), calls=%async_computation | async-start | bytes 1048576 | tf_op jit(solution)/shard_map/all_to_all | solution.py:213
  21.3 19.3 %copy-start.11 = (f32[3,128]{1,0:T(4,128)}, f32[3,128]{1,0:T(4,128)S(1)}, u32[]{:S(2)}) copy-start(f32[3,128]{1,0:T(4,128)S(1)} %add_rsqrt_fusion.3) | copy-start | bytes 4612
  40.5 6.7 %collective-permute-start = (bf16[4,16,2,8,128]{4,3,2,1,0:T(8,128)(2,1)}, bf16[4,16,2,8,128]{4,3,2,1,0:T(8,128)(2,1)}, u32[]{:S(2)}, u32[]{:S(2)}) collective-permute-start(bf16[4,16,2,8,128]{4,3,2,1,0:T(8,128)(2,1)} %get-tuple-element.22), channel_id=1, source_target_pairs={{0,64},{64,0},{1,65},{65,1},{2,66},{66,2},{3,67},{67,3},{4,68},{68... | collective-permute-start | bytes 786440 | tf_op jit(solution)/shard_map/ppermute | solution.py:216
  43.0 5.4 %copy-start.2 = (bf16[3,2,64,384]{3,2,0,1:T(8,128)(2,1)}, bf16[3,2,64,384]{3,2,0,1:T(8,128)(2,1)S(1)}, u32[]{:S(2)}) copy-start(bf16[3,2,64,384]{3,2,0,1:T(8,128)(2,1)S(1)} %copy.51) | copy-start | bytes 884740
  43.0 44.6 %collective-permute-start.1 = (bf16[2,3,64,384]{3,2,1,0:T(8,128)(2,1)S(1)}, bf16[2,3,64,384]{3,2,1,0:T(8,128)(2,1)}, u32[]{:S(2)}, u32[]{:S(2)}) collective-permute-start(bf16[2,3,64,384]{3,2,1,0:T(8,128)(2,1)S(1)} %bitcast.144), channel_id=1, source_target_pairs={{0,16},{16,32},{32,48},{48,0},{1,17},{17,33},{33,49},{49,1},{2,18}... | collective-permute-start | bytes 884744 | tf_op jit(solution)/shard_map/ppermute | solution.py:184
  43.8 49.9 %collective-permute-start.2 = (bf16[2,3,64,384]{3,2,1,0:T(8,128)(2,1)S(1)}, bf16[2,3,64,384]{3,2,1,0:T(8,128)(2,1)}, u32[]{:S(2)}, u32[]{:S(2)}) collective-permute-start(bf16[2,3,64,384]{3,2,1,0:T(8,128)(2,1)S(1)} %bitcast.145), channel_id=1, source_target_pairs={{0,48},{16,0},{32,16},{48,32},{1,49},{17,1},{33,17},{49,33},{2,50}... | collective-permute-start | bytes 884744 | tf_op jit(solution)/shard_map/ppermute | solution.py:185
  46.0 49.3 %collective-permute-start.7 = (bf16[192,768]{1,0:T(8,128)(2,1)}, bf16[192,768]{1,0:T(8,128)(2,1)}, u32[]{:S(2)}, u32[]{:S(2)}) collective-permute-start(bf16[192,768]{1,0:T(8,128)(2,1)} %param.22), channel_id=1, source_target_pairs={{0,128},{128,0},{1,129},{129,1},{2,130},{130,2},{3,131},{131,3},{4... | collective-permute-start | bytes 884744 | tf_op jit(solution)/shard_map/ppermute | solution.py:28
  48.2 1.0 copy-start.5
  48.2 11.2 %copy-start.12 = (f32[3,128]{1,0:T(4,128)S(1)}, f32[3,128]{1,0:T(4,128)}, u32[]{:S(2)}) copy-start(f32[3,128]{1,0:T(4,128)} %copy-done.11) | copy-start | bytes 4612
  50.2 24.6 %all-to-all-start.1 = ((bf16[128,8,128]{2,1,0:T(8,128)(2,1)}), bf16[128,8,128]{2,1,0:T(8,128)(2,1)S(1)}, u32[]{:S(2)}, u32[]{:S(2)}) async-start(bf16[128,8,128]{2,1,0:T(8,128)(2,1)} %bitcast.29), calls=%async_computation.1 | async-start | bytes 524288 | tf_op jit(solution)/shard_map/all_to_all | solution.py:229
  60.9 23.5 %copy-start.3 = (f32[3,192,128]{2,1,0:T(8,128)}, f32[3,192,128]{2,1,0:T(8,128)S(1)}, u32[]{:S(2)}) copy-start(f32[3,192,128]{2,1,0:T(8,128)S(1)} %fusion.18.refs_3_) | copy-start | bytes 884740
  61.0 14.2 %copy-start.10 = (bf16[128,128]{1,0:T(8,128)(2,1)S(1)}, bf16[128,128]{1,0:T(8,128)(2,1)}, u32[]{:S(2)}) copy-start(bf16[128,128]{1,0:T(8,128)(2,1)} %param.18) | copy-start | bytes 98308
  74.8 1.0 copy-start.6
  76.3 8.2 %copy-start.4 = (bf16[192,768]{1,0:T(8,128)(2,1)S(1)}, bf16[192,768]{1,0:T(8,128)(2,1)}, u32[]{:S(2)}) copy-start(bf16[192,768]{1,0:T(8,128)(2,1)} %param.22) | copy-start | bytes 884740
  77.6 19.5 %all-to-all-start.2 = ((f16[64,4,8,128]{3,2,1,0:T(8,128)(2,1)}), f16[64,4,8,128]{3,2,1,0:T(8,128)(2,1)S(1)}, u32[]{:S(2)}, u32[]{:S(2)}) async-start(f16[64,4,8,128]{3,2,1,0:T(8,128)(2,1)} %bitcast.49), calls=%async_computation.2 | async-start | bytes 1048576 | tf_op jit(solution)/shard_map/all_to_all | solution.py:247
  89.2 11.3 %collective-permute-start.3 = (bf16[3,64,384]{2,1,0:T(8,128)(2,1)}, bf16[3,64,384]{2,1,0:T(8,128)(2,1)S(1)}, u32[]{:S(2)}, u32[]{:S(2)}) collective-permute-start(bf16[3,64,384]{2,1,0:T(8,128)(2,1)} %slice_bitcast_fusion.2), channel_id=1, source_target_pairs={{0,16},{16,32},{32,48},{48,0},{1,17},{17,33},{33,49},{49,1},{2,18}... | collective-permute-start | bytes 442376 | tf_op jit(solution)/shard_map/ppermute | solution.py:187
  95.3 11.1 %collective-permute-start.4 = (bf16[3,64,384]{2,1,0:T(8,128)(2,1)}, bf16[3,64,384]{2,1,0:T(8,128)(2,1)}, u32[]{:S(2)}, u32[]{:S(2)}) collective-permute-start(bf16[3,64,384]{2,1,0:T(8,128)(2,1)} %slice_bitcast_fusion.1), channel_id=1, source_target_pairs={{0,48},{16,0},{32,16},{48,32},{1,49},{17,1},{33,17},{49,33},{2,50}... | collective-permute-start | bytes 442376 | tf_op jit(solution)/shard_map/ppermute | solution.py:188
  97.1 28.8 %collective-permute-start.8 = (bf16[384,768]{1,0:T(8,128)(2,1)}, bf16[384,768]{1,0:T(8,128)(2,1)}, u32[]{:S(2)}, u32[]{:S(2)}) collective-permute-start(bf16[384,768]{1,0:T(8,128)(2,1)} %pad_maximum_fusion), channel_id=1, source_target_pairs={{0,64},{64,0},{1,65},{65,1},{2,66},{66,2},{3,67},{67,3},{4,68},{68... | collective-permute-start | bytes 1769480 | tf_op jit(solution)/shard_map/ppermute | solution.py:30
  100.5 6.0 %copy-start.7 = (bf16[3,64,384]{2,1,0:T(8,128)(2,1)}, bf16[3,64,384]{2,1,0:T(8,128)(2,1)S(1)}, u32[]{:S(2)}) copy-start(bf16[3,64,384]{2,1,0:T(8,128)(2,1)S(1)} %collective-permute-done.3.refs_7_) | copy-start | bytes 442372
  111.7 14.3 %copy-start.8 = (bf16[3,192,128]{2,1,0:T(8,128)(2,1)S(1)}, bf16[3,192,128]{2,1,0:T(8,128)(2,1)}, u32[]{:S(2)}) copy-start(bf16[3,192,128]{2,1,0:T(8,128)(2,1)} %get-tuple-element.5) | copy-start | bytes 442372
  111.7 5.4 %collective-permute-start.5 = (bf16[3,192,128]{2,1,0:T(8,128)(2,1)}, bf16[3,192,128]{2,1,0:T(8,128)(2,1)S(1)}, u32[]{:S(2)}, u32[]{:S(2)}) collective-permute-start(bf16[3,192,128]{2,1,0:T(8,128)(2,1)} %get-tuple-element.5), channel_id=1, source_target_pairs={{0,128},{128,0},{1,129},{129,1},{2,130},{130,2},{3,131},{131,3},{4... | collective-permute-start | bytes 442376 | tf_op jit(solution)/shard_map/ppermute | solution.py:28
  118.0 8.0 %collective-permute-start.6 = (bf16[3,384,128]{2,1,0:T(8,128)(2,1)S(1)}, bf16[3,384,128]{2,1,0:T(8,128)(2,1)S(1)}, u32[]{:S(2)}, u32[]{:S(2)}) collective-permute-start(bf16[3,384,128]{2,1,0:T(8,128)(2,1)S(1)} %pad_maximum_fusion.2), channel_id=1, source_target_pairs={{0,64},{64,0},{1,65},{65,1},{2,66},{66,2},{3,67},{67,3},{4,68},{68... | collective-permute-start | bytes 884744 | tf_op jit(solution)/shard_map/ppermute | solution.py:30
  118.1 19.1 %all-to-all-start.3 = ((bf16[16,4,32,128]{3,2,1,0:T(8,128)(2,1)}), bf16[16,4,32,128]{3,2,1,0:T(8,128)(2,1)S(1)}, u32[]{:S(2)}, u32[]{:S(2)}) async-start(bf16[16,4,32,128]{3,2,1,0:T(8,128)(2,1)} %get-tuple-element.6), calls=%async_computation.3 | async-start | bytes 1048576 | tf_op jit(solution)/shard_map/all_to_all | solution.py:292

commit v3 on v2

--- a/solution.py
+++ b/solution.py
@@ -55,84 +55,89 @@
     pt,
     gacc,
 ):
-    samples, width, rows = qt_ref.shape
+    _, width, rows = qt_ref.shape
+    samples = top_ref.shape[0]
     row_count = 4
     scale = LOG2E / math.sqrt(head_size)
     row_at = row_ref[0]
-    qbd[...] = jnp.zeros_like(qbd)
-    dbd[...] = jnp.zeros_like(dbd)
-    gacc[...] = jnp.zeros_like(gacc)
+    s = pl.program_id(0)
+
+    @pl.when(s == 0)
+    def _():
+        qbd[...] = jnp.zeros_like(qbd)
+        dbd[...] = jnp.zeros_like(dbd)
+        gacc[...] = jnp.zeros_like(gacc)
+
     tiles = rows // 8
 
     def fold(x, op):
         return op(x.reshape(tiles, 8, 2 * rows), axis=0)
 
-    def one_sample(s, unused):
-        for step, halves in enumerate(
-            (
-                (own_ref.at[0], own_ref.at[1]),
-                (last_ref.at[0], last_ref.at[1]),
-                (top_ref, low_ref),
-                (next_ref.at[0], next_ref.at[1]),
+    for step, halves in enumerate(
+        (
+            (own_ref.at[0, 0], own_ref.at[1, 0]),
+            (last_ref.at[0, 0], last_ref.at[1, 0]),
+            (top_ref.at[s], low_ref.at[s]),
+            (next_ref.at[0, 0], next_ref.at[1, 0]),
+        )
+    ):
+        block = lax.rem(row_at + row_count - step, row_count)
+        for n, ref in enumerate(halves):
+            at = pl.multiple_of(block * rows + n * (rows // 2), rows // 2)
+            k_s[pl.ds(at, rows // 2), :] = ref[:, 0:width]
+            v_s[pl.ds(at, rows // 2), :] = ref[:, width : 2 * width]
+    for h in range(heads):
+        e0, i0 = h * head_size, h * rows
+        qbd[e0 : e0 + head_size, i0 : i0 + rows] = qt_ref[0, e0 : e0 + head_size, :]
+        dbd[e0 : e0 + head_size, i0 : i0 + rows] = dmt_ref[0, e0 : e0 + head_size, :]
+    for h in range(0, heads, 2):
+        lanes = slice(h * rows, (h + 2) * rows)
+        top = jnp.full((8, 2 * rows), -jnp.inf, F32)
+        for b in range(row_count):
+            part = slice(b * rows, (b + 1) * rows)
+            places = slice(b * tiles, (b + 1) * tiles)
+            bias = jnp.concatenate(
+                [bias_ref[places, h + n, :, :].reshape(rows, rows) for n in range(2)], axis=1
             )
-        ):
-            block = lax.rem(row_at + row_count - step, row_count)
-            for n, ref in enumerate(halves):
-                at = pl.multiple_of(block * rows + n * (rows // 2), rows // 2)
-                k_s[pl.ds(at, rows // 2), :] = ref[s, :, 0:width]
-                v_s[pl.ds(at, rows // 2), :] = ref[s, :, width : 2 * width]
+            x = jnp.dot(k_s[part, :], qbd[:, lanes], preferred_element_type=F32)
+            x = x * scale + bias
+            st[part, lanes] = x
+            top = jnp.maximum(top, fold(x, jnp.max))
+        peak = jnp.max(top, axis=0, keepdims=True)
+        total = jnp.zeros((8, 2 * rows), F32)
+        dots = jnp.zeros((8, 2 * rows), F32)
+        for b in range(row_count):
+            part = slice(b * rows, (b + 1) * rows)
+            d = jnp.dot(v_s[part, :], dbd[:, lanes], preferred_element_type=F32)
+            w = jnp.exp2(st[part, lanes] - peak)
+            st[part, lanes] = w
+            dpt[part, lanes] = d
+            total = total + fold(w, jnp.sum)
+            dots = dots + fold(w * d, jnp.sum)
+        inverse = 1.0 / jnp.sum(total, axis=0, keepdims=True)
+        inner = jnp.sum(dots, axis=0, keepdims=True) * inverse
+        for b in range(row_count):
+            part = slice(b * rows, (b + 1) * rows)
+            p = st[part, lanes] * inverse
+            pt[part, lanes] = p.astype(BF)
+            gacc[part, lanes] = gacc[part, lanes] + p * (dpt[part, lanes] - inner)
+    mixed = lax.dot_general(
+        v_s[...], pt[...], (((0,), (0,)), ((), ())), preferred_element_type=F32
+    )
+    for h in range(heads):
+        e0, i0 = h * head_size, h * rows
+        gated_ref[0, e0 : e0 + head_size, :] = (
+            mixed[e0 : e0 + head_size, i0 : i0 + rows] * gt_ref[0, e0 : e0 + head_size, :]
+        ).astype(BF)
+
+    @pl.when(s == samples - 1)
+    def _():
+        parts, _, width_j, _ = grad_ref.shape
         for h in range(heads):
-            e0, i0 = h * head_size, h * rows
-            qbd[e0 : e0 + head_size, i0 : i0 + rows] = qt_ref[s, e0 : e0 + head_size, :]
-            dbd[e0 : e0 + head_size, i0 : i0 + rows] = dmt_ref[s, e0 : e0 + head_size, :]
-        for h in range(0, heads, 2):
-            lanes = slice(h * rows, (h + 2) * rows)
-            top = jnp.full((8, 2 * rows), -jnp.inf, F32)
-            for b in range(row_count):
-                part = slice(b * rows, (b + 1) * rows)
-                places = slice(b * tiles, (b + 1) * tiles)
-                bias = jnp.concatenate(
-                    [bias_ref[places, h + n, :, :].reshape(rows, rows) for n in range(2)], axis=1
-                )
-                x = jnp.dot(k_s[part, :], qbd[:, lanes], preferred_element_type=F32)
-                x = x * scale + bias
-                st[part, lanes] = x
-                top = jnp.maximum(top, fold(x, jnp.max))
-            peak = jnp.max(top, axis=0, keepdims=True)
-            total = jnp.zeros((8, 2 * rows), F32)
-            dots = jnp.zeros((8, 2 * rows), F32)
-            for b in range(row_count):
-                part = slice(b * rows, (b + 1) * rows)
-                d = jnp.dot(v_s[part, :], dbd[:, lanes], preferred_element_type=F32)
-                w = jnp.exp2(st[part, lanes] - peak)
-                st[part, lanes] = w
-                dpt[part, lanes] = d
-                total = total + fold(w, jnp.sum)
-                dots = dots + fold(w * d, jnp.sum)
-            inverse = 1.0 / jnp.sum(total, axis=0, keepdims=True)
-            inner = jnp.sum(dots, axis=0, keepdims=True) * inverse
-            for b in range(row_count):
-                part = slice(b * rows, (b + 1) * rows)
-                p = st[part, lanes] * inverse
-                pt[part, lanes] = p.astype(BF)
-                gacc[part, lanes] = gacc[part, lanes] + p * (dpt[part, lanes] - inner)
-        mixed = lax.dot_general(
-            v_s[...], pt[...], (((0,), (0,)), ((), ())), preferred_element_type=F32
-        )
-        for h in range(heads):
-            e0, i0 = h * head_size, h * rows
-            gated_ref[s, e0 : e0 + head_size, :] = (
-                mixed[e0 : e0 + head_size, i0 : i0 + rows] * gt_ref[s, e0 : e0 + head_size, :]
-            ).astype(BF)
-        return unused
-
-    lax.fori_loop(0, samples, one_sample, 0)
-    parts, _, width_j, _ = grad_ref.shape
-    for h in range(heads):
-        for c in range(parts):
-            grad_ref[c, h, :, :] = gacc[
-                c * width_j : (c + 1) * width_j, h * rows : (h + 1) * rows
-            ].astype(BF)
+            for c in range(parts):
+                grad_ref[c, h, :, :] = gacc[
+                    c * width_j : (c + 1) * width_j, h * rows : (h + 1) * rows
+                ].astype(BF)
 
 
 def on_device(
@@ -230,6 +235,9 @@
     tri_local = tri_local.reshape(channels, col_width, tok_rows)
     out_normed = normalize(tri_local.astype(F32), 0).astype(BF)
     bias_scaled = lax.optimization_barrier(bias_weight * LOG2E)
+    key_tile = lax.optimization_barrier(
+        jnp.broadcast_to((mask_cols == 1).astype(F32)[:, None], (col_width, tok_rows))
+    )
     gate_out = jax.nn.sigmoid(
         jnp.einsum("jic,cd->jid", normed, proj_in[:, 4 * channels :], preferred_element_type=F32)
     )
@@ -239,7 +247,7 @@
     bias_local = jnp.einsum(
         "jic,ch->hji", normalize(pair_new, 2), bias_scaled, precision=lax.Precision.HIGHEST
     )
-    bias_local = jnp.where((mask_cols == 1)[None, :, None], bias_local, HIDDEN).astype(jnp.float16)
+    bias_local = jnp.where(key_tile[None] > 0.5, bias_local, HIDDEN).astype(jnp.float16)
     copies = jnp.broadcast_to(
         bias_local.reshape(grp_count, 1, heads, col_width, tok_rows),
         (grp_count, col_count, heads, col_width, tok_rows),
@@ -257,14 +265,23 @@
     weights = gather_grp(w_out, 0)
     keys = row_count * tok_rows
     vmem = pl.BlockSpec(memory_space=pltpu.VMEM)
+    by_sample = pl.BlockSpec((1, head_width, tok_rows), lambda s: (s, 0, 0))
+    of_tokens = pl.BlockSpec((2, 1, tok_rows // 2, 2 * head_width), lambda s: (0, s, 0, 0))
     gated_t, grads = pl.pallas_call(
         lambda *refs: attention_kernel(heads, head_size, *refs),
         out_shape=(
-            jax.ShapeDtypeStruct((samples, head_width, tok_rows), BF),
-            jax.ShapeDtypeStruct((col_count, heads, keys // col_count, tok_rows), BF),
+            pltpu.VMEM((samples, head_width, tok_rows), BF),
+            pltpu.VMEM((col_count, heads, keys // col_count, tok_rows), BF),
         ),
-        in_specs=[pl.BlockSpec(memory_space=pltpu.SMEM)] + [vmem] * 9,
-        out_specs=(vmem, vmem),
+        compiler_params=pltpu.CompilerParams(
+            vmem_limit_bytes=24 << 20, dimension_semantics=("arbitrary",)
+        ),
+        grid=(samples,),
+        in_specs=[pl.BlockSpec(memory_space=pltpu.SMEM)]
+        + [by_sample] * 3
+        + [of_tokens] * 3
+        + [vmem] * 3,
+        out_specs=(by_sample, vmem),
         scratch_shapes=[
             pltpu.VMEM((keys, head_width), BF),
             pltpu.VMEM((keys, head_width), BF),
@@ -278,14 +295,19 @@
         name="attention",
     )(
         row_at.astype(jnp.int32).reshape(1),
-        query_t,
-        d_mixed_t,
-        gate_t,
-        key_value,
-        from_last,
-        from_next,
-        far_top,
-        far_low,
+        *[
+            pltpu.with_memory_space_constraint(value, pltpu.HBM)
+            for value in (
+                query_t,
+                d_mixed_t,
+                gate_t,
+                key_value,
+                from_last,
+                from_next,
+            )
+        ],
+        pltpu.with_memory_space_constraint(far_top, pltpu.VMEM),
+        pltpu.with_memory_space_constraint(far_low, pltpu.VMEM),
         pltpu.with_memory_space_constraint(bias_all, pltpu.VMEM),
     )
     gated_parts = gather_grp(gated_t, 1)

time: 139 us -> 123 us (0.88)
  the two profiles are of different devices: /device:TPU:64 before, /device:TPU:2 now
where the time goes in v3:
time: 123 us; the launch traced here: 121 us
  starting transfers between devices  47.1 us (38%)
  waiting for transfers between devices  40 us (33%)
  matrix products  13 us (11%)
  local copies, waits for them, and re-layouts  8.36 us (7%)
  other arithmetic  6.2 us (5%)
  Pallas kernels  5.09 us (4%)
    all_to_all x1, starting transfers between devices, on_device(): got = lax.all_to_all(send, everywhere, 0, 0, tiled=True)  15.4 us
    all_to_all x1, waiting for transfers between devices, on_device(): got = lax.all_to_all(send, everywhere, 0, 0, tiled=True)  12.5 us
    all_to_all x1, waiting for transfers between devices, on_device(): tri_local = lax.all_to_all(back, everywhere, 0, 0, tiled=True)  11.3 us
    all_to_all x1, starting transfers between devices, on_device(): grad_parts = lax.all_to_all(grads, 'col', 0, 0, tiled=True)  7.28 us
    all_to_all x1, starting transfers between devices, on_device(): tri_local = lax.all_to_all(back, everywhere, 0, 0, tiled=True)  7.03 us
    all_to_all x1, waiting for transfers between devices, on_device(): grad_parts = lax.all_to_all(grads, 'col', 0, 0, tiled=True)  6.39 us
    all_to_all x1, starting transfers between devices, on_device(): bias_all = lax.all_to_all(copies, ('near', 'core', 'col'), 0, 0, tiled=True)  5.7 us
    pallas_call x1, Pallas kernels, on_device(): pl.pallas_call(lambda *refs: attention_kernel(heads, head_size, *refs), o...  5.09 us
  transfers between devices with their start and end apart: 13, of which 8 were waited for; matrix products, arithmetic and copies ran while one was open for 17% of the time, Pallas kernels for 4%

profile of v3, /device:TPU:2, one launch (start us, length us, event | category | flops | bytes accessed | tf_op | source)
XLA Modules:
  0.0 120.7 jit_solution(9556691030729285393)
XLA Ops:
  0.7 0.8 pad_add_fusion
  1.6 1.1 copy.42
  2.8 1.0 fusion.75
  4.8 1.2 copy.46
  6.0 15.4 %all-to-all-start = ((bf16[128,16,128]{2,1,0:T(8,128)(2,1)}), bf16[128,16,128]{2,1,0:T(8,128)(2,1)S(1)}, u32[]{:S(2)}, u32[]{:S(2)}) async-start(bf16[128,16,128]{2,1,0:T(8,128)(2,1)} %copy.46), calls=%async_computation | async-start | bytes 1048576 | tf_op jit(solution)/shard_map/all_to_all | solution.py:218
  24.2 2.6 %collective-permute-start.1 = (bf16[2,3,64,384]{3,2,1,0:T(8,128)(2,1)S(1)}, bf16[2,3,64,384]{3,2,1,0:T(8,128)(2,1)S(1)}, u32[]{:S(2)}, u32[]{:S(2)}) collective-permute-start(bf16[2,3,64,384]{3,2,1,0:T(8,128)(2,1)S(1)} %bitcast.144), channel_id=1, source_target_pairs={{0,16},{16,32},{32,48},{48,0},{1,17},{17,33},{33,49},{49,1},{2,18}... | collective-permute-start | bytes 884744 | tf_op jit(solution)/shard_map/ppermute | solution.py:189
  26.8 1.7 %collective-permute-start.2 = (bf16[2,3,64,384]{3,2,1,0:T(8,128)(2,1)S(1)}, bf16[2,3,64,384]{3,2,1,0:T(8,128)(2,1)}, u32[]{:S(2)}, u32[]{:S(2)}) collective-permute-start(bf16[2,3,64,384]{3,2,1,0:T(8,128)(2,1)S(1)} %bitcast.145), channel_id=1, source_target_pairs={{0,48},{16,0},{32,16},{48,32},{1,49},{17,1},{33,17},{49,33},{2,50}... | collective-permute-start | bytes 884744 | tf_op jit(solution)/shard_map/ppermute | solution.py:190
  28.5 1.3 %collective-permute-start.7 = (bf16[192,768]{1,0:T(8,128)(2,1)}, bf16[192,768]{1,0:T(8,128)(2,1)}, u32[]{:S(2)}, u32[]{:S(2)}) collective-permute-start(bf16[192,768]{1,0:T(8,128)(2,1)} %param.22), channel_id=1, source_target_pairs={{0,128},{128,0},{1,129},{129,1},{2,130},{130,2},{3,131},{131,3},{4... | collective-permute-start | bytes 884744 | tf_op jit(solution)/shard_map/ppermute | solution.py:28
  29.9 12.5 %all-to-all-done = bf16[128,16,128]{2,1,0:T(8,128)(2,1)S(1)} async-done(((bf16[128,16,128]{2,1,0:T(8,128)(2,1)}), bf16[128,16,128]{2,1,0:T(8,128)(2,1)S(1)}, u32[]{:S(2)}, u32[]{:S(2)}) %all-to-all-start) | async-done | bytes 524320 | tf_op jit(solution)/shard_map/all_to_all | solution.py:218
  43.3 1.8 %collective-permute-done = bf16[4,16,2,8,128]{4,3,2,1,0:T(8,128)(2,1)} collective-permute-done((bf16[4,16,2,8,128]{4,3,2,1,0:T(8,128)(2,1)}, bf16[4,16,2,8,128]{4,3,2,1,0:T(8,128)(2,1)}, u32[]{:S(2)}, u32[]{:S(2)}) %collective-permute-start) | collective-permute-done | bytes 262176 | tf_op jit(solution)/shard_map/ppermute | solution.py:221
  45.1 1.0 select_bitcast_fusion.1
  46.2 1.1 fusion.7
  47.3 7.0 %all-to-all-start.1 = ((bf16[128,8,128]{2,1,0:T(8,128)(2,1)}), bf16[128,8,128]{2,1,0:T(8,128)(2,1)S(1)}, u32[]{:S(2)}, u32[]{:S(2)}) async-start(bf16[128,8,128]{2,1,0:T(8,128)(2,1)} %bitcast.29), calls=%async_computation.1 | async-start | bytes 524288 | tf_op jit(solution)/shard_map/all_to_all | solution.py:234
  54.4 1.5 %fusion.18.refs_3_ = f32[3,192,128]{2,1,0:T(8,128)S(1)} fusion(bf16[3,128,768]{2,1,0:T(8,128)(2,1)S(1)} %copy-done.1, f32[3,128]{1,0:T(4,128)S(1)} %add_rsqrt_fusion.3, f32[3,128]{1,0:T(4,128)S(1)} %broadcast_multiply_fusion.4, bf16[4,768,192]{1,2,0:T(8,128)(2,1)} %param.21), kind=kOutput, calls=%fused_computation.30 | convolution fusion | flops 114647040 | bytes 1182720 | tf_op jit(solution)/shard_map/srd,de->ser/dot_general | solution.py:261
  55.8 2.0 %fusion.5 = f32[8,128,128]{1,2,0:T(8,128)} fusion(f32[8,128]{1,0:T(8,128)S(1)} %add_rsqrt_fusion.2, f32[8,128]{1,0:T(8,128)S(1)} %broadcast_multiply_fusion.3, bf16[128,640]{1,0:T(8,128)(2,1)} %param.17, f32[8,128,128]{1,2,0:T(8,128)S(1)} %get-tuple-element.31, bf16[128,8,128]{0,2,1:T(8,128)(2,1)S(1)} %copy.42), kind=kOutput, calls=%fused_computation.12 | convolution fusion | flops 34603008 | bytes 1351680 | tf_op jit(solution)/shard_map/jic,cd->jid/dot_general | solution.py:242
  57.8 11.3 %all-to-all-done.1 = bf16[128,8,128]{2,1,0:T(8,128)(2,1)S(1)} async-done(((bf16[128,8,128]{2,1,0:T(8,128)(2,1)}), bf16[128,8,128]{2,1,0:T(8,128)(2,1)S(1)}, u32[]{:S(2)}, u32[]{:S(2)}) %all-to-all-start.1) | async-done | bytes 262176 | tf_op jit(solution)/shard_map/all_to_all | solution.py:234
  71.1 0.9 broadcast_in_dim.66
  72.0 5.7 %all-to-all-start.2 = ((f16[64,4,8,128]{3,2,1,0:T(8,128)(2,1)}), f16[64,4,8,128]{3,2,1,0:T(8,128)(2,1)S(1)}, u32[]{:S(2)}, u32[]{:S(2)}) async-start(f16[64,4,8,128]{3,2,1,0:T(8,128)(2,1)} %bitcast.49), calls=%async_computation.2 | async-start | bytes 1048576 | tf_op jit(solution)/shard_map/all_to_all | solution.py:255
  77.7 1.0 fusion.19.refs_2_
  78.8 2.1 %fusion.20.refs_1_ = bf16[3,192,128]{2,1,0:T(8,128)(2,1)} fusion(bf16[3,128,768]{2,1,0:T(8,128)(2,1)S(1)} %copy-done.1, f32[3,128]{1,0:T(4,128)S(1)} %add_rsqrt_fusion.3, f32[3,128]{1,0:T(4,128)S(1)} %broadcast_multiply_fusion.4, bf16[4,768,192]{1,2,0:T(8,128)(2,1)} %param.21), kind=kOutput, calls=%fused_computation.33 | convolution fusion | flops 114499584 | bytes 1035264 | tf_op jit(solution)/shard_map/srd,de->ser/dot_general | solution.py:259
  81.7 0.9 slice_bitcast_fusion.1
  82.6 3.5 %collective-permute-start.4 = (bf16[3,64,384]{2,1,0:T(8,128)(2,1)S(1)}, bf16[3,64,384]{2,1,0:T(8,128)(2,1)S(1)}, u32[]{:S(2)}, u32[]{:S(2)}) collective-permute-start(bf16[3,64,384]{2,1,0:T(8,128)(2,1)S(1)} %slice_bitcast_fusion.1), channel_id=1, source_target_pairs={{0,48},{16,0},{32,16},{48,32},{1,49},{17,1},{33,17},{49,33},{2,50}... | collective-permute-start | bytes 442376 | tf_op jit(solution)/shard_map/ppermute | solution.py:193
  86.1 1.8 %pad_maximum_fusion = bf16[384,768]{1,0:T(8,128)(2,1)} fusion(bf16[192,768]{1,0:T(8,128)(2,1)} %collective-permute-done.7, bf16[192,768]{1,0:T(8,128)(2,1)S(1)} %copy-done.4), kind=kLoop, calls=%fused_computation.48 | loop fusion | flops 1179648 | bytes 1179648 | tf_op jit(solution)/shard_map/concatenate | solution.py:29
  87.9 1.2 all-to-all-done.2
  89.2 2.9 %collective-permute-done.3.refs_7_ = bf16[3,64,384]{2,1,0:T(8,128)(2,1)S(1)} collective-permute-done((bf16[3,64,384]{2,1,0:T(8,128)(2,1)S(1)}, bf16[3,64,384]{2,1,0:T(8,128)(2,1)S(1)}, u32[]{:S(2)}, u32[]{:S(2)}) %collective-permute-start.3) | collective-permute-done | bytes 147488 | tf_op jit(solution)/shard_map/ppermute | solution.py:192
  92.5 5.1 %attention.1 = (bf16[3,192,128]{2,1,0:T(8,128)(2,1)S(1)}, bf16[16,4,32,128]{3,2,1,0:T(8,128)(2,1)}) custom-call(s32[1]{0:T(128)} %bitcast.32.refs_0_, bf16[3,192,128]{2,1,0:T(8,128)(2,1)} %fusion.20.refs_1_, bf16[3,192,128]{2,1,0:T(8,128)(2,1)} %fusion.19.refs_2_, f32[3,192,128]{2,1,0:T(8,128)} %copy-done.3, bf16[2,3,64,384]{3,2,1,0:T(8,128)(2,1)} %bitcast.146, ...), custom_call_target="tpu_custom_call" | custom-call | tf_op jit(solution)/shard_map/attention/pallas_call | solution.py:270
  97.6 1.6 %collective-permute-start.5 = (bf16[3,192,128]{2,1,0:T(8,128)(2,1)S(1)}, bf16[3,192,128]{2,1,0:T(8,128)(2,1)S(1)}, u32[]{:S(2)}, u32[]{:S(2)}) collective-permute-start(bf16[3,192,128]{2,1,0:T(8,128)(2,1)S(1)} %get-tuple-element.5), channel_id=1, source_target_pairs={{0,128},{128,0},{1,129},{129,1},{2,130},{130,2},{3,131},{131,3},{4... | collective-permute-start | bytes 442376 | tf_op jit(solution)/shard_map/ppermute | solution.py:28
  99.2 3.6 %collective-permute-done.5 = bf16[3,192,128]{2,1,0:T(8,128)(2,1)S(1)} collective-permute-done((bf16[3,192,128]{2,1,0:T(8,128)(2,1)S(1)}, bf16[3,192,128]{2,1,0:T(8,128)(2,1)S(1)}, u32[]{:S(2)}, u32[]{:S(2)}) %collective-permute-start.5) | collective-permute-done | bytes 147488 | tf_op jit(solution)/shard_map/ppermute | solution.py:28
  102.9 7.3 %all-to-all-start.3 = ((bf16[16,4,32,128]{3,2,1,0:T(8,128)(2,1)}), bf16[16,4,32,128]{3,2,1,0:T(8,128)(2,1)S(1)}, u32[]{:S(2)}, u32[]{:S(2)}) async-start(bf16[16,4,32,128]{3,2,1,0:T(8,128)(2,1)} %get-tuple-element.6), calls=%async_computation.3 | async-start | bytes 1048576 | tf_op jit(solution)/shard_map/all_to_all | solution.py:314
  110.1 0.9 copy.55
  111.0 2.6 %fusion.2 = bf16[3,128,768]{2,1,0:T(8,128)(2,1)} fusion(bf16[3,128,768]{2,1,0:T(8,128)(2,1)S(1)} %copy-done.1, bf16[384,768]{1,0:T(8,128)(2,1)} %collective-permute-done.8, bf16[192,768]{1,0:T(8,128)(2,1)} %collective-permute-done.7, bf16[192,768]{1,0:T(8,128)(2,1)S(1)} %copy-done.4, bf16[3,384,128]{2,1,0:T(8,128)(2,1)S(1)} %collective-permute-done.6, ...), kind=kOutput, calls=%fused_computation.7 | convolution fusion | flops 459177984 | bytes 2949120 | tf_op jit(solution)/shard_map/ser,ed->srd/dot_general | solution.py:317
  113.6 6.4 %all-to-all-done.3 = bf16[16,4,32,128]{3,2,1,0:T(8,128)(2,1)S(1)} async-done(((bf16[16,4,32,128]{3,2,1,0:T(8,128)(2,1)}), bf16[16,4,32,128]{3,2,1,0:T(8,128)(2,1)S(1)}, u32[]{:S(2)}, u32[]{:S(2)}) %all-to-all-start.3) | async-done | bytes 524320 | tf_op jit(solution)/shard_map/all_to_all | solution.py:314
  (76 shorter events, 8.9 us)
Async XLA Ops:
  0.6 77.1 %copy-start = (bf16[3,128,768]{2,1,0:T(8,128)(2,1)S(1)}, bf16[3,128,768]{2,1,0:T(8,128)(2,1)}, u32[]{:S(2)}) copy-start(bf16[3,128,768]{2,1,0:T(8,128)(2,1)} %param.23) | copy-start | bytes 1769476
  0.6 3.3 %copy-start.7 = (bf16[128,640]{1,0:T(8,128)(2,1)S(1)}, bf16[128,640]{1,0:T(8,128)(2,1)}, u32[]{:S(2)}) copy-start(bf16[128,640]{1,0:T(8,128)(2,1)} %param.17) | copy-start | bytes 491524
  4.8 16.7 %copy-start.1 = (bf16[3,128,768]{2,1,0:T(8,128)(2,1)S(1)}, bf16[3,128,768]{2,1,0:T(8,128)(2,1)}, u32[]{:S(2)}) copy-start(bf16[3,128,768]{2,1,0:T(8,128)(2,1)} %param.20) | copy-start | bytes 1769476
  6.0 36.4 %all-to-all-start = ((bf16[128,16,128]{2,1,0:T(8,128)(2,1)}), bf16[128,16,128]{2,1,0:T(8,128)(2,1)S(1)}, u32[]{:S(2)}, u32[]{:S(2)}) async-start(bf16[128,16,128]{2,1,0:T(8,128)(2,1)} %copy.46), calls=%async_computation | async-start | bytes 1048576 | tf_op jit(solution)/shard_map/all_to_all | solution.py:218
  21.5 1.3 %copy-start.10 = (bf16[4,768,192]{1,2,0:T(8,128)(2,1)S(1)}, bf16[4,768,192]{1,2,0:T(8,128)(2,1)}, u32[]{:S(2)}) copy-start(bf16[4,768,192]{1,2,0:T(8,128)(2,1)} %param.21) | copy-start | bytes 3538948
  23.6 19.6 %copy-start.9 = (f32[128,16]{0,1:T(8,128)S(1)}, f32[128,16]{0,1:T(8,128)}, u32[]{:S(2)}) copy-start(f32[128,16]{0,1:T(8,128)} %param.19) | copy-start | bytes 24580
  24.2 21.9 %copy-start.2 = (bf16[3,2,64,384]{3,2,0,1:T(8,128)(2,1)}, bf16[3,2,64,384]{3,2,0,1:T(8,128)(2,1)S(1)}, u32[]{:S(2)}) copy-start(bf16[3,2,64,384]{3,2,0,1:T(8,128)(2,1)S(1)} %copy.51) | copy-start | bytes 884740
  24.2 56.6 %collective-permute-start.1 = (bf16[2,3,64,384]{3,2,1,0:T(8,128)(2,1)S(1)}, bf16[2,3,64,384]{3,2,1,0:T(8,128)(2,1)S(1)}, u32[]{:S(2)}, u32[]{:S(2)}) collective-permute-start(bf16[2,3,64,384]{3,2,1,0:T(8,128)(2,1)S(1)} %bitcast.144), channel_id=1, source_target_pairs={{0,16},{16,32},{32,48},{48,0},{1,17},{17,33},{33,49},{49,1},{2,18}... | collective-permute-start | bytes 884744 | tf_op jit(solution)/shard_map/ppermute | solution.py:189
  26.8 54.8 %collective-permute-start.2 = (bf16[2,3,64,384]{3,2,1,0:T(8,128)(2,1)S(1)}, bf16[2,3,64,384]{3,2,1,0:T(8,128)(2,1)}, u32[]{:S(2)}, u32[]{:S(2)}) collective-permute-start(bf16[2,3,64,384]{3,2,1,0:T(8,128)(2,1)S(1)} %bitcast.145), channel_id=1, source_target_pairs={{0,48},{16,0},{32,16},{48,32},{1,49},{17,1},{33,17},{49,33},{2,50}... | collective-permute-start | bytes 884744 | tf_op jit(solution)/shard_map/ppermute | solution.py:190
  28.5 57.6 %collective-permute-start.7 = (bf16[192,768]{1,0:T(8,128)(2,1)}, bf16[192,768]{1,0:T(8,128)(2,1)}, u32[]{:S(2)}, u32[]{:S(2)}) collective-permute-start(bf16[192,768]{1,0:T(8,128)(2,1)} %param.22), channel_id=1, source_target_pairs={{0,128},{128,0},{1,129},{129,1},{2,130},{130,2},{3,131},{131,3},{4... | collective-permute-start | bytes 884744 | tf_op jit(solution)/shard_map/ppermute | solution.py:28
  43.2 1.9 %collective-permute-start = (bf16[4,16,2,8,128]{4,3,2,1,0:T(8,128)(2,1)}, bf16[4,16,2,8,128]{4,3,2,1,0:T(8,128)(2,1)}, u32[]{:S(2)}, u32[]{:S(2)}) collective-permute-start(bf16[4,16,2,8,128]{4,3,2,1,0:T(8,128)(2,1)} %get-tuple-element.22), channel_id=1, source_target_pairs={{0,64},{64,0},{1,65},{65,1},{2,66},{66,2},{3,67},{67,3},{4,68},{68... | collective-permute-start | bytes 786440 | tf_op jit(solution)/shard_map/ppermute | solution.py:221
  47.3 21.8 %all-to-all-start.1 = ((bf16[128,8,128]{2,1,0:T(8,128)(2,1)}), bf16[128,8,128]{2,1,0:T(8,128)(2,1)S(1)}, u32[]{:S(2)}, u32[]{:S(2)}) async-start(bf16[128,8,128]{2,1,0:T(8,128)(2,1)} %bitcast.29), calls=%async_computation.1 | async-start | bytes 524288 | tf_op jit(solution)/shard_map/all_to_all | solution.py:234
  55.8 21.9 %copy-start.3 = (f32[3,192,128]{2,1,0:T(8,128)}, f32[3,192,128]{2,1,0:T(8,128)S(1)}, u32[]{:S(2)}) copy-start(f32[3,192,128]{2,1,0:T(8,128)S(1)} %fusion.18.refs_3_) | copy-start | bytes 884740
  55.8 13.7 %copy-start.8 = (bf16[128,128]{1,0:T(8,128)(2,1)S(1)}, bf16[128,128]{1,0:T(8,128)(2,1)}, u32[]{:S(2)}) copy-start(bf16[128,128]{1,0:T(8,128)(2,1)} %param.18) | copy-start | bytes 98308
  69.1 1.0 copy-start.6
  70.7 7.1 %copy-start.4 = (bf16[192,768]{1,0:T(8,128)(2,1)S(1)}, bf16[192,768]{1,0:T(8,128)(2,1)}, u32[]{:S(2)}) copy-start(bf16[192,768]{1,0:T(8,128)(2,1)} %param.22) | copy-start | bytes 884740
  72.0 17.1 %all-to-all-start.2 = ((f16[64,4,8,128]{3,2,1,0:T(8,128)(2,1)}), f16[64,4,8,128]{3,2,1,0:T(8,128)(2,1)S(1)}, u32[]{:S(2)}, u32[]{:S(2)}) async-start(f16[64,4,8,128]{3,2,1,0:T(8,128)(2,1)} %bitcast.49), calls=%async_computation.2 | async-start | bytes 1048576 | tf_op jit(solution)/shard_map/all_to_all | solution.py:255
  80.9 8.4 %copy-start.5 = (bf16[2,3,64,384]{3,2,1,0:T(8,128)(2,1)}, bf16[2,3,64,384]{3,2,1,0:T(8,128)(2,1)S(1)}, u32[]{:S(2)}) copy-start(bf16[2,3,64,384]{3,2,1,0:T(8,128)(2,1)S(1)} %collective-permute-done.1.refs_5_) | copy-start | bytes 884740
  80.9 11.3 %collective-permute-start.3 = (bf16[3,64,384]{2,1,0:T(8,128)(2,1)S(1)}, bf16[3,64,384]{2,1,0:T(8,128)(2,1)S(1)}, u32[]{:S(2)}, u32[]{:S(2)}) collective-permute-start(bf16[3,64,384]{2,1,0:T(8,128)(2,1)S(1)} %slice_bitcast_fusion.2), channel_id=1, source_target_pairs={{0,16},{16,32},{32,48},{48,0},{1,17},{17,33},{33,49},{49,1},{2,18}... | collective-permute-start | bytes 442376 | tf_op jit(solution)/shard_map/ppermute | solution.py:192
  82.6 9.9 %collective-permute-start.4 = (bf16[3,64,384]{2,1,0:T(8,128)(2,1)S(1)}, bf16[3,64,384]{2,1,0:T(8,128)(2,1)S(1)}, u32[]{:S(2)}, u32[]{:S(2)}) collective-permute-start(bf16[3,64,384]{2,1,0:T(8,128)(2,1)S(1)} %slice_bitcast_fusion.1), channel_id=1, source_target_pairs={{0,48},{16,0},{32,16},{48,32},{1,49},{17,1},{33,17},{49,33},{2,50}... | collective-permute-start | bytes 442376 | tf_op jit(solution)/shard_map/ppermute | solution.py:193
  87.9 23.1 %collective-permute-start.8 = (bf16[384,768]{1,0:T(8,128)(2,1)}, bf16[384,768]{1,0:T(8,128)(2,1)}, u32[]{:S(2)}, u32[]{:S(2)}) collective-permute-start(bf16[384,768]{1,0:T(8,128)(2,1)} %pad_maximum_fusion), channel_id=1, source_target_pairs={{0,64},{64,0},{1,65},{65,1},{2,66},{66,2},{3,67},{67,3},{4,68},{68... | collective-permute-start | bytes 1769480 | tf_op jit(solution)/shard_map/ppermute | solution.py:30
  97.6 5.1 %collective-permute-start.5 = (bf16[3,192,128]{2,1,0:T(8,128)(2,1)S(1)}, bf16[3,192,128]{2,1,0:T(8,128)(2,1)S(1)}, u32[]{:S(2)}, u32[]{:S(2)}) collective-permute-start(bf16[3,192,128]{2,1,0:T(8,128)(2,1)S(1)} %get-tuple-element.5), channel_id=1, source_target_pairs={{0,128},{128,0},{1,129},{129,1},{2,130},{130,2},{3,131},{131,3},{4... | collective-permute-start | bytes 442376 | tf_op jit(solution)/shard_map/ppermute | solution.py:28
  102.8 8.3 %collective-permute-start.6 = (bf16[3,384,128]{2,1,0:T(8,128)(2,1)S(1)}, bf16[3,384,128]{2,1,0:T(8,128)(2,1)S(1)}, u32[]{:S(2)}, u32[]{:S(2)}) collective-permute-start(bf16[3,384,128]{2,1,0:T(8,128)(2,1)S(1)} %pad_maximum_fusion.2), channel_id=1, source_target_pairs={{0,64},{64,0},{1,65},{65,1},{2,66},{66,2},{3,67},{67,3},{4,68},{68... | collective-permute-start | bytes 884744 | tf_op jit(solution)/shard_map/ppermute | solution.py:30
  102.9 17.2 %all-to-all-start.3 = ((bf16[16,4,32,128]{3,2,1,0:T(8,128)(2,1)}), bf16[16,4,32,128]{3,2,1,0:T(8,128)(2,1)S(1)}, u32[]{:S(2)}, u32[]{:S(2)}) async-start(bf16[16,4,32,128]{3,2,1,0:T(8,128)(2,1)} %get-tuple-element.6), calls=%async_computation.3 | async-start | bytes 1048576 | tf_op jit(solution)/shard_map/all_to_all | solution.py:314

commit v4 on v3

--- a/solution.py
+++ b/solution.py
@@ -262,7 +262,10 @@
     )
     back_t = jnp.einsum("srd,ed->ser", cotangent, w_out, preferred_element_type=F32)
     d_mixed_t = (back_t * gate_t).astype(BF)
-    weights = gather_grp(w_out, 0)
+    w_far = lax.ppermute(w_out, "near", SWAP)
+    w_near = lax.ppermute(w_out, "core", SWAP)
+    w_both = lax.ppermute(w_far, "core", SWAP)
+    weights = jnp.concatenate([w_out, w_far, w_near, w_both], axis=0)
     keys = row_count * tok_rows
     vmem = pl.BlockSpec(memory_space=pltpu.VMEM)
     by_sample = pl.BlockSpec((1, head_width, tok_rows), lambda s: (s, 0, 0))

time: 123 us -> 137 us (1.11)
  the two profiles are of different devices: /device:TPU:2 before, /device:TPU:64 now
where the time goes in v4:
time: 137 us; the launch traced here: 136 us
  waiting for transfers between devices  56.2 us (41%)
  starting transfers between devices  46.5 us (34%)
  matrix products  13.2 us (10%)
  local copies, waits for them, and re-layouts  9.41 us (7%)
  other arithmetic  5.08 us (4%)
  Pallas kernels  5.06 us (4%)
    all_to_all x1, waiting for transfers between devices, on_device(): got = lax.all_to_all(send, everywhere, 0, 0, tiled=True)  18.4 us
    all_to_all x1, starting transfers between devices, on_device(): got = lax.all_to_all(send, everywhere, 0, 0, tiled=True)  14.7 us
    all_to_all x1, waiting for transfers between devices, on_device(): tri_local = lax.all_to_all(back, everywhere, 0, 0, tiled=True)  14.1 us
    all_to_all x1, starting transfers between devices, on_device(): tri_local = lax.all_to_all(back, everywhere, 0, 0, tiled=True)  9.29 us
    all_to_all x1, waiting for transfers between devices, on_device(): grad_parts = lax.all_to_all(grads, 'col', 0, 0, tiled=True)  8.71 us
    all_to_all x1, starting transfers between devices, on_device(): grad_parts = lax.all_to_all(grads, 'col', 0, 0, tiled=True)  6.98 us
    all_to_all x1, starting transfers between devices, on_device(): bias_all = lax.all_to_all(copies, ('near', 'core', 'col'), 0, 0, tiled=True)  6.64 us
    ppermute x1, waiting for transfers between devices, on_device(): far_low = lax.ppermute(next_half, 'row', backward)  5.37 us
  transfers between devices with their start and end apart: 14, of which 7 were waited for; matrix products, arithmetic and copies ran while one was open for 14% of the time, Pallas kernels for 4%

profile of v4, /device:TPU:64, one launch (start us, length us, event | category | flops | bytes accessed | tf_op | source)
XLA Modules:
  0.0 136.5 jit_solution(8235927056027271551)
XLA Ops:
  0.7 0.8 pad_add_fusion
  1.6 1.1 copy.42
  2.8 1.0 fusion.77
  4.8 1.2 copy.46
  6.0 14.7 %all-to-all-start = ((bf16[128,16,128]{2,1,0:T(8,128)(2,1)}), bf16[128,16,128]{2,1,0:T(8,128)(2,1)S(1)}, u32[]{:S(2)}, u32[]{:S(2)}) async-start(bf16[128,16,128]{2,1,0:T(8,128)(2,1)} %copy.46), calls=%async_computation | async-start | bytes 1048576 | tf_op jit(solution)/shard_map/all_to_all | solution.py:218
  21.3 18.4 %all-to-all-done = bf16[128,16,128]{2,1,0:T(8,128)(2,1)S(1)} async-done(((bf16[128,16,128]{2,1,0:T(8,128)(2,1)}), bf16[128,16,128]{2,1,0:T(8,128)(2,1)S(1)}, u32[]{:S(2)}, u32[]{:S(2)}) %all-to-all-start) | async-done | bytes 524320 | tf_op jit(solution)/shard_map/all_to_all | solution.py:218
  39.6 0.9 slice_bitcast_fusion
  40.5 1.7 %fusion.6 = bf16[3,128,2,192]{1,3,2,0:T(8,128)(2,1)S(1)} fusion(bf16[4,768,192]{1,2,0:T(8,128)(2,1)} %param.21, bf16[3,128,768]{2,1,0:T(8,128)(2,1)S(1)} %copy-done.1, f32[3,128]{1,0:T(4,128)S(1)} %add_rsqrt_fusion.3, f32[3,128]{1,0:T(4,128)S(1)} %broadcast_multiply_fusion.4, pred[128,2]{0,1:T(4,128)(4,1)S(1)} %broadcast_or_fusion), kind=kOutput, calls=%fused_computation.15 | convolution fusion | flops 227966976 | bytes 1477888 | tf_op jit(solution)/shard_map/srd,tde->srte/dot_general | solution.py:180
  43.0 0.8 collective-permute-start.1
  43.8 2.2 %collective-permute-start.2 = (bf16[2,3,64,384]{3,2,1,0:T(8,128)(2,1)S(1)}, bf16[2,3,64,384]{3,2,1,0:T(8,128)(2,1)}, u32[]{:S(2)}, u32[]{:S(2)}) collective-permute-start(bf16[2,3,64,384]{3,2,1,0:T(8,128)(2,1)S(1)} %bitcast.145), channel_id=1, source_target_pairs={{0,48},{16,0},{32,16},{48,32},{1,49},{17,1},{33,17},{49,33},{2,50}... | collective-permute-start | bytes 884744 | tf_op jit(solution)/shard_map/ppermute | solution.py:190
  47.2 1.0 select_bitcast_fusion.1
  49.1 1.0 fusion.7
  50.2 9.3 %all-to-all-start.1 = ((bf16[128,8,128]{2,1,0:T(8,128)(2,1)}), bf16[128,8,128]{2,1,0:T(8,128)(2,1)S(1)}, u32[]{:S(2)}, u32[]{:S(2)}) async-start(bf16[128,8,128]{2,1,0:T(8,128)(2,1)} %bitcast.29), calls=%async_computation.1 | async-start | bytes 524288 | tf_op jit(solution)/shard_map/all_to_all | solution.py:234
  59.5 1.1 fusion.5
  60.7 14.1 %all-to-all-done.1 = bf16[128,8,128]{2,1,0:T(8,128)(2,1)S(1)} async-done(((bf16[128,8,128]{2,1,0:T(8,128)(2,1)}), bf16[128,8,128]{2,1,0:T(8,128)(2,1)S(1)}, u32[]{:S(2)}, u32[]{:S(2)}) %all-to-all-start.1) | async-done | bytes 262176 | tf_op jit(solution)/shard_map/all_to_all | solution.py:234
  76.8 0.9 broadcast_in_dim.66
  77.6 6.6 %all-to-all-start.2 = ((f16[64,4,8,128]{3,2,1,0:T(8,128)(2,1)}), f16[64,4,8,128]{3,2,1,0:T(8,128)(2,1)S(1)}, u32[]{:S(2)}, u32[]{:S(2)}) async-start(f16[64,4,8,128]{3,2,1,0:T(8,128)(2,1)} %bitcast.49), calls=%async_computation.2 | async-start | bytes 1048576 | tf_op jit(solution)/shard_map/all_to_all | solution.py:255
  84.3 1.5 %fusion.20.refs_3_ = f32[3,192,128]{2,1,0:T(8,128)S(1)} fusion(bf16[3,128,768]{2,1,0:T(8,128)(2,1)S(1)} %copy-done.1, f32[3,128]{1,0:T(4,128)S(1)} %copy-done.10, f32[3,128]{1,0:T(4,128)S(1)} %broadcast_multiply_fusion.4, bf16[4,768,192]{1,2,0:T(8,128)(2,1)} %param.21), kind=kOutput, calls=%fused_computation.32 | convolution fusion | flops 114647040 | bytes 1182720 | tf_op jit(solution)/shard_map/srd,de->ser/dot_general | solution.py:261
  85.8 1.0 fusion.21.refs_2_
  86.9 2.1 %fusion.22.refs_1_ = bf16[3,192,128]{2,1,0:T(8,128)(2,1)} fusion(bf16[3,128,768]{2,1,0:T(8,128)(2,1)S(1)} %copy-done.1, f32[3,128]{1,0:T(4,128)S(1)} %copy-done.10, f32[3,128]{1,0:T(4,128)S(1)} %broadcast_multiply_fusion.4, bf16[4,768,192]{1,2,0:T(8,128)(2,1)} %param.21), kind=kOutput, calls=%fused_computation.35 | convolution fusion | flops 114499584 | bytes 1035264 | tf_op jit(solution)/shard_map/srd,de->ser/dot_general | solution.py:259
  89.0 0.9 slice_bitcast_fusion.2
  89.9 4.6 %collective-permute-start.3 = (bf16[3,64,384]{2,1,0:T(8,128)(2,1)S(1)}, bf16[3,64,384]{2,1,0:T(8,128)(2,1)S(1)}, u32[]{:S(2)}, u32[]{:S(2)}) collective-permute-start(bf16[3,64,384]{2,1,0:T(8,128)(2,1)S(1)} %slice_bitcast_fusion.2), channel_id=1, source_target_pairs={{0,16},{16,32},{32,48},{48,0},{1,17},{17,33},{33,49},{49,1},{2,18}... | collective-permute-start | bytes 442376 | tf_op jit(solution)/shard_map/ppermute | solution.py:192
  94.5 0.9 slice_bitcast_fusion.1
  95.5 1.2 all-to-all-done.2
  96.9 4.0 %collective-permute-done.3.refs_7_ = bf16[3,64,384]{2,1,0:T(8,128)(2,1)S(1)} collective-permute-done((bf16[3,64,384]{2,1,0:T(8,128)(2,1)S(1)}, bf16[3,64,384]{2,1,0:T(8,128)(2,1)S(1)}, u32[]{:S(2)}, u32[]{:S(2)}) %collective-permute-start.3) | collective-permute-done | bytes 147488 | tf_op jit(solution)/shard_map/ppermute | solution.py:192
  100.9 5.4 %collective-permute-done.4.refs_8_ = bf16[3,64,384]{2,1,0:T(8,128)(2,1)S(1)} collective-permute-done((bf16[3,64,384]{2,1,0:T(8,128)(2,1)S(1)}, bf16[3,64,384]{2,1,0:T(8,128)(2,1)S(1)}, u32[]{:S(2)}, u32[]{:S(2)}) %collective-permute-start.4) | collective-permute-done | bytes 147488 | tf_op jit(solution)/shard_map/ppermute | solution.py:193
  106.3 5.1 %attention.1 = (bf16[3,192,128]{2,1,0:T(8,128)(2,1)S(1)}, bf16[16,4,32,128]{3,2,1,0:T(8,128)(2,1)}) custom-call(s32[1]{0:T(128)} %bitcast.32.refs_0_, bf16[3,192,128]{2,1,0:T(8,128)(2,1)} %fusion.22.refs_1_, bf16[3,192,128]{2,1,0:T(8,128)(2,1)} %fusion.21.refs_2_, f32[3,192,128]{2,1,0:T(8,128)} %copy-done.3, bf16[2,3,64,384]{3,2,1,0:T(8,128)(2,1)} %bitcast.146, ...), custom_call_target="tpu_custom_call" | custom-call | tf_op jit(solution)/shard_map/attention/pallas_call | solution.py:273
  112.1 4.4 %collective-permute-done.5 = bf16[3,192,128]{2,1,0:T(8,128)(2,1)S(1)} collective-permute-done((bf16[3,192,128]{2,1,0:T(8,128)(2,1)S(1)}, bf16[3,192,128]{2,1,0:T(8,128)(2,1)S(1)}, u32[]{:S(2)}, u32[]{:S(2)}) %collective-permute-start.5) | collective-permute-done | bytes 147488 | tf_op jit(solution)/shard_map/ppermute | solution.py:28
  116.6 7.0 %all-to-all-start.3 = ((bf16[16,4,32,128]{3,2,1,0:T(8,128)(2,1)}), bf16[16,4,32,128]{3,2,1,0:T(8,128)(2,1)S(1)}, u32[]{:S(2)}, u32[]{:S(2)}) async-start(bf16[16,4,32,128]{3,2,1,0:T(8,128)(2,1)} %get-tuple-element.6), calls=%async_computation.3 | async-start | bytes 1048576 | tf_op jit(solution)/shard_map/all_to_all | solution.py:317
  123.6 0.9 copy.55
  124.5 2.5 %fusion.2 = bf16[3,128,768]{2,1,0:T(8,128)(2,1)} fusion(bf16[3,128,768]{2,1,0:T(8,128)(2,1)S(1)} %copy-done.1, bf16[192,768]{1,0:T(8,128)(2,1)} %collective-permute-done.9, bf16[192,768]{1,0:T(8,128)(2,1)S(1)} %collective-permute-done.8, bf16[192,768]{1,0:T(8,128)(2,1)S(1)} %collective-permute-done.7, bf16[192,768]{1,0:T(8,128)(2,1)S(1)} %copy-done.6, ...), kind=kOutput, calls=%fused_computation.7 | convolution fusion | flops 460357632 | bytes 2949120 | tf_op jit(solution)/shard_map/ser,ed->srd/dot_general | solution.py:320
  127.1 8.7 %all-to-all-done.3 = bf16[16,4,32,128]{3,2,1,0:T(8,128)(2,1)S(1)} async-done(((bf16[16,4,32,128]{3,2,1,0:T(8,128)(2,1)}), bf16[16,4,32,128]{3,2,1,0:T(8,128)(2,1)S(1)}, u32[]{:S(2)}, u32[]{:S(2)}) %all-to-all-start.3) | async-done | bytes 524320 | tf_op jit(solution)/shard_map/all_to_all | solution.py:317
  (77 shorter events, 8.4 us)
Async XLA Ops:
  0.6 85.2 %copy-start = (bf16[3,128,768]{2,1,0:T(8,128)(2,1)S(1)}, bf16[3,128,768]{2,1,0:T(8,128)(2,1)}, u32[]{:S(2)}) copy-start(bf16[3,128,768]{2,1,0:T(8,128)(2,1)} %param.23) | copy-start | bytes 1769476
  0.6 3.3 %copy-start.7 = (bf16[128,640]{1,0:T(8,128)(2,1)S(1)}, bf16[128,640]{1,0:T(8,128)(2,1)}, u32[]{:S(2)}) copy-start(bf16[128,640]{1,0:T(8,128)(2,1)} %param.17) | copy-start | bytes 491524
  4.8 15.9 %copy-start.1 = (bf16[3,128,768]{2,1,0:T(8,128)(2,1)S(1)}, bf16[3,128,768]{2,1,0:T(8,128)(2,1)}, u32[]{:S(2)}) copy-start(bf16[3,128,768]{2,1,0:T(8,128)(2,1)} %param.20) | copy-start | bytes 1769476
  6.0 33.6 %all-to-all-start = ((bf16[128,16,128]{2,1,0:T(8,128)(2,1)}), bf16[128,16,128]{2,1,0:T(8,128)(2,1)S(1)}, u32[]{:S(2)}, u32[]{:S(2)}) async-start(bf16[128,16,128]{2,1,0:T(8,128)(2,1)} %copy.46), calls=%async_computation | async-start | bytes 1048576 | tf_op jit(solution)/shard_map/all_to_all | solution.py:218
  21.3 19.3 %copy-start.9 = (f32[3,128]{1,0:T(4,128)}, f32[3,128]{1,0:T(4,128)S(1)}, u32[]{:S(2)}) copy-start(f32[3,128]{1,0:T(4,128)S(1)} %add_rsqrt_fusion.3) | copy-start | bytes 4612
  40.5 6.7 %collective-permute-start = (bf16[4,16,2,8,128]{4,3,2,1,0:T(8,128)(2,1)}, bf16[4,16,2,8,128]{4,3,2,1,0:T(8,128)(2,1)}, u32[]{:S(2)}, u32[]{:S(2)}) collective-permute-start(bf16[4,16,2,8,128]{4,3,2,1,0:T(8,128)(2,1)} %get-tuple-element.22), channel_id=1, source_target_pairs={{0,64},{64,0},{1,65},{65,1},{2,66},{66,2},{3,67},{67,3},{4,68},{68... | collective-permute-start | bytes 786440 | tf_op jit(solution)/shard_map/ppermute | solution.py:221
  43.0 5.3 %copy-start.2 = (bf16[3,2,64,384]{3,2,0,1:T(8,128)(2,1)}, bf16[3,2,64,384]{3,2,0,1:T(8,128)(2,1)S(1)}, u32[]{:S(2)}) copy-start(bf16[3,2,64,384]{3,2,0,1:T(8,128)(2,1)S(1)} %copy.51) | copy-start | bytes 884740
  43.0 45.9 %collective-permute-start.1 = (bf16[2,3,64,384]{3,2,1,0:T(8,128)(2,1)S(1)}, bf16[2,3,64,384]{3,2,1,0:T(8,128)(2,1)}, u32[]{:S(2)}, u32[]{:S(2)}) collective-permute-start(bf16[2,3,64,384]{3,2,1,0:T(8,128)(2,1)S(1)} %bitcast.144), channel_id=1, source_target_pairs={{0,16},{16,32},{32,48},{48,0},{1,17},{17,33},{33,49},{49,1},{2,18}... | collective-permute-start | bytes 884744 | tf_op jit(solution)/shard_map/ppermute | solution.py:189
  43.8 50.7 %collective-permute-start.2 = (bf16[2,3,64,384]{3,2,1,0:T(8,128)(2,1)S(1)}, bf16[2,3,64,384]{3,2,1,0:T(8,128)(2,1)}, u32[]{:S(2)}, u32[]{:S(2)}) collective-permute-start(bf16[2,3,64,384]{3,2,1,0:T(8,128)(2,1)S(1)} %bitcast.145), channel_id=1, source_target_pairs={{0,48},{16,0},{32,16},{48,32},{1,49},{17,1},{33,17},{49,33},{2,50}... | collective-permute-start | bytes 884744 | tf_op jit(solution)/shard_map/ppermute | solution.py:190
  46.0 65.6 %collective-permute-start.7 = (bf16[192,768]{1,0:T(8,128)(2,1)}, bf16[192,768]{1,0:T(8,128)(2,1)S(1)}, u32[]{:S(2)}, u32[]{:S(2)}) collective-permute-start(bf16[192,768]{1,0:T(8,128)(2,1)} %param.22), channel_id=1, source_target_pairs={{0,128},{128,0},{1,129},{129,1},{2,130},{130,2},{3,131},{131,3},{4... | collective-permute-start | bytes 884744 | tf_op jit(solution)/shard_map/ppermute | solution.py:265
  48.2 1.0 copy-start.4
  50.2 24.6 %all-to-all-start.1 = ((bf16[128,8,128]{2,1,0:T(8,128)(2,1)}), bf16[128,8,128]{2,1,0:T(8,128)(2,1)S(1)}, u32[]{:S(2)}, u32[]{:S(2)}) async-start(bf16[128,8,128]{2,1,0:T(8,128)(2,1)} %bitcast.29), calls=%async_computation.1 | async-start | bytes 524288 | tf_op jit(solution)/shard_map/all_to_all | solution.py:234
  59.5 15.6 %copy-start.8 = (bf16[128,128]{1,0:T(8,128)(2,1)S(1)}, bf16[128,128]{1,0:T(8,128)(2,1)}, u32[]{:S(2)}) copy-start(bf16[128,128]{1,0:T(8,128)(2,1)} %param.18) | copy-start | bytes 98308
  74.8 1.0 copy-start.5
  76.3 8.0 %copy-start.10 = (f32[3,128]{1,0:T(4,128)S(1)}, f32[3,128]{1,0:T(4,128)}, u32[]{:S(2)}) copy-start(f32[3,128]{1,0:T(4,128)} %copy-done.9) | copy-start | bytes 4612
  77.6 19.1 %all-to-all-start.2 = ((f16[64,4,8,128]{3,2,1,0:T(8,128)(2,1)}), f16[64,4,8,128]{3,2,1,0:T(8,128)(2,1)S(1)}, u32[]{:S(2)}, u32[]{:S(2)}) async-start(f16[64,4,8,128]{3,2,1,0:T(8,128)(2,1)} %bitcast.49), calls=%async_computation.2 | async-start | bytes 1048576 | tf_op jit(solution)/shard_map/all_to_all | solution.py:255
  84.3 1.5 %copy-start.6 = (bf16[192,768]{1,0:T(8,128)(2,1)S(1)}, bf16[192,768]{1,0:T(8,128)(2,1)}, u32[]{:S(2)}) copy-start(bf16[192,768]{1,0:T(8,128)(2,1)} %param.22) | copy-start | bytes 884740
  85.8 3.1 %copy-start.3 = (f32[3,192,128]{2,1,0:T(8,128)}, f32[3,192,128]{2,1,0:T(8,128)S(1)}, u32[]{:S(2)}) copy-start(f32[3,192,128]{2,1,0:T(8,128)S(1)} %fusion.20.refs_3_) | copy-start | bytes 884740
  89.9 11.0 %collective-permute-start.3 = (bf16[3,64,384]{2,1,0:T(8,128)(2,1)S(1)}, bf16[3,64,384]{2,1,0:T(8,128)(2,1)S(1)}, u32[]{:S(2)}, u32[]{:S(2)}) collective-permute-start(bf16[3,64,384]{2,1,0:T(8,128)(2,1)S(1)} %slice_bitcast_fusion.2), channel_id=1, source_target_pairs={{0,16},{16,32},{32,48},{48,0},{1,17},{17,33},{33,49},{49,1},{2,18}... | collective-permute-start | bytes 442376 | tf_op jit(solution)/shard_map/ppermute | solution.py:192
  95.4 10.9 %collective-permute-start.4 = (bf16[3,64,384]{2,1,0:T(8,128)(2,1)S(1)}, bf16[3,64,384]{2,1,0:T(8,128)(2,1)S(1)}, u32[]{:S(2)}, u32[]{:S(2)}) collective-permute-start(bf16[3,64,384]{2,1,0:T(8,128)(2,1)S(1)} %slice_bitcast_fusion.1), channel_id=1, source_target_pairs={{0,48},{16,0},{32,16},{48,32},{1,49},{17,1},{33,17},{49,33},{2,50}... | collective-permute-start | bytes 442376 | tf_op jit(solution)/shard_map/ppermute | solution.py:193
  111.4 5.1 %collective-permute-start.5 = (bf16[3,192,128]{2,1,0:T(8,128)(2,1)S(1)}, bf16[3,192,128]{2,1,0:T(8,128)(2,1)S(1)}, u32[]{:S(2)}, u32[]{:S(2)}) collective-permute-start(bf16[3,192,128]{2,1,0:T(8,128)(2,1)S(1)} %get-tuple-element.5), channel_id=1, source_target_pairs={{0,128},{128,0},{1,129},{129,1},{2,130},{130,2},{3,131},{131,3},{4... | collective-permute-start | bytes 442376 | tf_op jit(solution)/shard_map/ppermute | solution.py:28
  111.6 12.9 %collective-permute-start.8 = (bf16[192,768]{1,0:T(8,128)(2,1)S(1)}, bf16[192,768]{1,0:T(8,128)(2,1)S(1)}, u32[]{:S(2)}, u32[]{:S(2)}) collective-permute-start(bf16[192,768]{1,0:T(8,128)(2,1)S(1)} %copy-done.6), channel_id=1, source_target_pairs={{0,64},{64,0},{1,65},{65,1},{2,66},{66,2},{3,67},{67,3},{4,68},{68... | collective-permute-start | bytes 884744 | tf_op jit(solution)/shard_map/ppermute | solution.py:266
  111.6 12.9 %collective-permute-start.9 = (bf16[192,768]{1,0:T(8,128)(2,1)S(1)}, bf16[192,768]{1,0:T(8,128)(2,1)}, u32[]{:S(2)}, u32[]{:S(2)}) collective-permute-start(bf16[192,768]{1,0:T(8,128)(2,1)S(1)} %collective-permute-done.7), channel_id=1, source_target_pairs={{0,64},{64,0},{1,65},{65,1},{2,66},{66,2},{3,67},{67,3},{4,68},{68... | collective-permute-start | bytes 884744 | tf_op jit(solution)/shard_map/ppermute | solution.py:267
  116.5 8.0 %collective-permute-start.6 = (bf16[3,384,128]{2,1,0:T(8,128)(2,1)S(1)}, bf16[3,384,128]{2,1,0:T(8,128)(2,1)}, u32[]{:S(2)}, u32[]{:S(2)}) collective-permute-start(bf16[3,384,128]{2,1,0:T(8,128)(2,1)S(1)} %pad_maximum_fusion.1), channel_id=1, source_target_pairs={{0,64},{64,0},{1,65},{65,1},{2,66},{66,2},{3,67},{67,3},{4,68},{68... | collective-permute-start | bytes 884744 | tf_op jit(solution)/shard_map/ppermute | solution.py:30
  116.6 19.1 %all-to-all-start.3 = ((bf16[16,4,32,128]{3,2,1,0:T(8,128)(2,1)}), bf16[16,4,32,128]{3,2,1,0:T(8,128)(2,1)S(1)}, u32[]{:S(2)}, u32[]{:S(2)}) async-start(bf16[16,4,32,128]{3,2,1,0:T(8,128)(2,1)} %get-tuple-element.6), calls=%async_computation.3 | async-start | bytes 1048576 | tf_op jit(solution)/shard_map/all_to_all | solution.py:317
